TPU v7x, 256 devices: a whole 4x4x8 slice. The times are simulated.
256 devices in a mesh: gz: 32 (over y, z_hi, core), gy: 8 (over z_lo, x).
Axes of the slice: x: 4, y: 4, z: 8 (z_hi: 4, z_lo: 2; z = z_hi * 2 + z_lo), core: 2. Of those that a mesh axis runs over, the one named last changes fastest.
Arguments:
- estimate: float32 [512, 256, 512], P('gz', 'gy'), may hold values from 0.5 to 2
- measured: float32 [4, 512, 256, 512], P(None, 'gz', 'gy'), may hold values from 0.25 to 4
- psf_z: float32 [4, 31], replicated, may hold values from 0.1 to 1
- psf_y: float32 [4, 15], replicated, may hold values from 0.1 to 1
- psf_x: float32 [4, 15], replicated, may hold values from 0.1 to 1
- extents: int32 [4, 3], replicated, may hold values from 9 to 31, as said below
- order: int32 [4], replicated, may hold values from 0 to 3, each once
Outputs:
- updated: float32 [512, 256, 512], P('gz', 'gy')
Inputs may be any that keep to these rules, and one draw needn't show every extreme that they name: `extents`: every extent is odd; along z it lies in 9 to 31, along y and x in 9 to 15; in every draw some view has extent 31 along z and some view has extent 15 along y.
All inputs are finite; a program needn't handle non-finite values.
Results may differ from a plain program's by a relative error of at most 0.0001.
Values sent between devices are 32-bit elements; how exact they have to be, the bound alone decides.
No kernel may reach another device: no remote copies, remote signals or barrier semaphores. Data moves between devices by JAX's collectives and lax.ppermute only.
A program may use at most 64 MiB of HBM per device.

v0:
```python
import jax
import jax.numpy as jnp
from jax import lax
from jax.sharding import PartitionSpec as P


def with_halo(value, sides, width):
    for axis, dim in sides:
        size, length = (lax.axis_size(axis), value.shape[dim])
        up = [(i, (i + 1) % size) for i in range(size - 1)]
        down = [(j, i) for i, j in up]
        last = lax.slice_in_dim(value, length - width, length, axis=dim)
        initial = lax.slice_in_dim(value, 0, width, axis=dim)
        before = lax.ppermute(last, axis, up)
        after = lax.ppermute(initial, axis, down)
        value = jnp.concatenate([before, value, after], axis=dim)
    return value


def line_taps(profile, reach_cells, tap_reach):
    offsets = jnp.arange(2 * tap_reach + 1, dtype=jnp.int32) - tap_reach
    kept = jnp.where(jnp.abs(offsets) <= reach_cells, profile, jnp.zeros_like(profile))
    return kept / jnp.sum(kept)


def correlate_padded(padded, weights, along_axis, tap_reach, length, flipped):
    total = None
    for offset in range(2 * tap_reach + 1):
        start = 2 * tap_reach - offset if flipped else offset
        piece = lax.slice_in_dim(padded, start, start + length, axis=along_axis)
        term = weights[offset] * piece
        total = term if total is None else total + term
    return total


def blur(field, weights_z, weights_y, weights_x, flipped):
    planes = field.shape[0]
    rows = field.shape[1]
    padded = with_halo(field, (("gz", 0),), 15)
    result = correlate_padded(padded, weights_z, 0, 15, planes, flipped)
    widened = with_halo(result, (("gy", 1),), 7)
    result = correlate_padded(widened, weights_y, 1, 7, rows, flipped)
    result = jnp.pad(result, ((0, 0), (0, 0), (7, 7)))
    return correlate_padded(result, weights_x, 2, 7, field.shape[2], flipped)


def on_device(estimate, measured, psf_z, psf_y, psf_x, extents, order):
    current = estimate
    for position in range(measured.shape[0]):
        view = order[position]
        radii = (extents[view] - 1) // 2
        weights_z = line_taps(psf_z[view], radii[0], 15)
        weights_y = line_taps(psf_y[view], radii[1], 7)
        weights_x = line_taps(psf_x[view], radii[2], 7)
        recorded = lax.dynamic_index_in_dim(measured, view, 0, keepdims=False)
        blurred = blur(current, weights_z, weights_y, weights_x, False)
        ratio = recorded / blurred
        current = current * blur(ratio, weights_z, weights_y, weights_x, True)
    return current


def solution(mesh):
    return jax.shard_map(
        on_device,
        mesh=mesh,
        in_specs=(P("gz", "gy", None), P(None, "gz", "gy", None), P(), P(), P(), P(), P()),
        out_specs=P("gz", "gy", None),
        check_vma=False,
    )
```

profile of v0, /device:TPU:30, one launch (start us, length us, event | category | flops | bytes accessed | tf_op | source)
XLA Modules:
  0.0 745.0 jit_solution(15281260050211416409)
XLA Ops:
  36.5 23.4 %fusion.1168 = f32[16,32,512]{2,1,0:T(8,128)S(1)} fusion(f32[31,32,512]{2,1,0:T(8,128)S(1)} %constant_dynamic-update-slice_fusion.2, f32[31,32,512]{2,1,0:T(8,128)S(1)} %get-tuple-element.59, f32[16,32,512]{2,1,0:T(8,128)S(1)} %copy-done, f32[]{:T(128)} %bitcast.41, f32[]{:T(128)} %bitcast.40, f32[]{:T(128)} %bitcast.39, f32[]{:T(128)} %bitcast.38, ...), kind=kLoop, calls=%fused_computation.1895 | loop fusion | flops 15990784 | bytes 33554556 | tf_op jit(solution)/shard_map/add | solution.py:32
  84.5 14.4 %fusion.319 = f32[16,32,512]{2,1,0:T(8,128)S(1)} fusion(f32[16,32,512]{2,1,0:T(8,128)S(1)} %fusion.269, f32[4,16,32,512]{3,2,1,0:T(8,128)} %param.8, s32[]{:T(128)S(6)} %select_n.81, f32[]{:T(128)} %bitcast.69, f32[]{:T(128)} %bitcast.68, f32[]{:T(128)} %bitcast.67, f32[]{:T(128)} %bitcast.66, f32[]{:T(128)} %bitcast.65, f32[]{:T(128)} %bitcast.64, ...), kind=kLoop, calls=%fused_computation.1015 | loop fusion | flops 7864320 | bytes 3145792 | tf_op jit(solution)/shard_map/div | solution.py:57
  107.7 18.8 %collective-permute-done.5 = f32[15,32,512]{2,1,0:T(8,128)S(1)} collective-permute-done((f32[15,32,512]{2,1,0:T(8,128)S(1)}, f32[15,32,512]{2,1,0:T(8,128)S(1)}, u32[]{:S(2)}, u32[]{:S(2)}) %collective-permute-start.5) | collective-permute-done | bytes 983072 | tf_op jit(solution)/shard_map/ppermute | solution.py:14
  127.6 23.4 %fusion.1055 = f32[16,32,512]{2,1,0:T(8,128)S(1)} fusion(f32[16,32,512]{2,1,0:T(8,128)S(1)} %fusion.319, f32[15,32,512]{2,1,0:T(8,128)S(1)} %collective-permute-done.5, f32[15,32,512]{2,1,0:T(8,128)S(1)} %collective-permute-done.4, f32[]{:T(128)} %bitcast.41, f32[]{:T(128)} %bitcast.40, f32[]{:T(128)} %bitcast.39, f32[]{:T(128)} %bitcast.38, f32[]{:T(128)} %bitcast.37, ...), kind=kLoop, calls=%fused_computation.1751 | loop fusion | flops 23855104 | bytes 4063356 | tf_op jit(solution)/shard_map/add | solution.py:32
  176.9 13.3 %fusion.348 = f32[16,32,512]{2,1,0:T(8,128)S(1)} fusion(f32[16,32,512]{2,1,0:T(8,128)S(1)} %copy-done, f32[16,32,512]{2,1,0:T(8,128)S(1)} %fusion.231, f32[]{:T(128)} %bitcast.69, f32[]{:T(128)} %bitcast.68, f32[]{:T(128)} %bitcast.67, f32[]{:T(128)} %bitcast.66, f32[]{:T(128)} %bitcast.65, f32[]{:T(128)} %bitcast.64, f32[]{:T(128)} %bitcast.63, ...), kind=kLoop, calls=%fused_computation.1044 | loop fusion | flops 7864320 | bytes 3145788 | tf_op jit(solution)/shard_map/mul | solution.py:58
  218.0 23.5 %fusion.969 = f32[16,32,512]{2,1,0:T(8,128)S(1)} fusion(f32[16,32,512]{2,1,0:T(8,128)S(1)} %fusion.348, f32[15,32,512]{2,1,0:T(8,128)S(1)} %collective-permute-done.9, f32[15,32,512]{2,1,0:T(8,128)S(1)} %collective-permute-done.8, f32[]{:T(128)} %bitcast.111, f32[]{:T(128)} %bitcast.110, f32[]{:T(128)} %bitcast.109, f32[]{:T(128)} %bitcast.108, ...), kind=kLoop, calls=%fused_computation.1665 | loop fusion | flops 23855104 | bytes 4063356 | tf_op jit(solution)/shard_map/add | solution.py:32
  269.2 14.3 %fusion.377 = f32[16,32,512]{2,1,0:T(8,128)S(1)} fusion(f32[16,32,512]{2,1,0:T(8,128)S(1)} %fusion.193, f32[4,16,32,512]{3,2,1,0:T(8,128)} %param.8, s32[]{:T(128)S(6)} %select_n.86, f32[]{:T(128)} %bitcast.139, f32[]{:T(128)} %bitcast.138, f32[]{:T(128)} %bitcast.137, f32[]{:T(128)} %bitcast.136, f32[]{:T(128)} %bitcast.135, f32[]{:T(128)} %bitcast.134, ...), kind=kLoop, calls=%fused_computation.1073 | loop fusion | flops 7864320 | bytes 3145792 | tf_op jit(solution)/shard_map/div | solution.py:57
  292.3 19.0 %collective-permute-done.13 = f32[15,32,512]{2,1,0:T(8,128)S(1)} collective-permute-done((f32[15,32,512]{2,1,0:T(8,128)S(1)}, f32[15,32,512]{2,1,0:T(8,128)S(1)}, u32[]{:S(2)}, u32[]{:S(2)}) %collective-permute-start.13) | collective-permute-done | bytes 983072 | tf_op jit(solution)/shard_map/ppermute | solution.py:14
  314.4 23.5 %fusion.883 = f32[16,32,512]{2,1,0:T(8,128)S(1)} fusion(f32[16,32,512]{2,1,0:T(8,128)S(1)} %fusion.377, f32[15,32,512]{2,1,0:T(8,128)S(1)} %collective-permute-done.13, f32[15,32,512]{2,1,0:T(8,128)S(1)} %collective-permute-done.12, f32[]{:T(128)} %bitcast.111, f32[]{:T(128)} %bitcast.110, f32[]{:T(128)} %bitcast.109, f32[]{:T(128)} %bitcast.108, ...), kind=kLoop, calls=%fused_computation.1579 | loop fusion | flops 23855104 | bytes 4063356 | tf_op jit(solution)/shard_map/add | solution.py:32
  350.2 11.9 %fusion.155 = f32[16,32,512]{2,1,0:T(8,128)S(1)} fusion(f32[16,32,512]{2,1,0:T(8,128)S(1)} %fusion.883, f32[16,7,512]{2,1,0:T(8,128)S(1)} %collective-permute-done.15, f32[16,7,512]{2,1,0:T(8,128)S(1)} %collective-permute-done.14, f32[]{:T(128)} %bitcast.125, f32[]{:T(128)} %bitcast.124, f32[]{:T(128)} %bitcast.123, f32[]{:T(128)} %bitcast.122, ...), kind=kLoop, calls=%fused_computation.851 | loop fusion | flops 11272192 | bytes 2555964 | tf_op jit(solution)/shard_map/add | solution.py:32
  362.1 13.2 %fusion.406 = f32[16,32,512]{2,1,0:T(8,128)S(1)} fusion(f32[16,32,512]{2,1,0:T(8,128)S(1)} %fusion.348, f32[16,32,512]{2,1,0:T(8,128)S(1)} %fusion.155, f32[]{:T(128)} %bitcast.139, f32[]{:T(128)} %bitcast.138, f32[]{:T(128)} %bitcast.137, f32[]{:T(128)} %bitcast.136, f32[]{:T(128)} %bitcast.135, f32[]{:T(128)} %bitcast.134, f32[]{:T(128)} %bitcast.133, ...), kind=kLoop, calls=%fused_computation.1102 | loop fusion | flops 7864320 | bytes 3145788 | tf_op jit(solution)/shard_map/mul | solution.py:58
  386.5 16.4 %collective-permute-done.17 = f32[15,32,512]{2,1,0:T(8,128)S(1)} collective-permute-done((f32[15,32,512]{2,1,0:T(8,128)S(1)}, f32[15,32,512]{2,1,0:T(8,128)S(1)}, u32[]{:S(2)}, u32[]{:S(2)}) %collective-permute-start.17) | collective-permute-done | bytes 983072 | tf_op jit(solution)/shard_map/ppermute | solution.py:15
  406.4 23.5 %fusion.797 = f32[16,32,512]{2,1,0:T(8,128)S(1)} fusion(f32[16,32,512]{2,1,0:T(8,128)S(1)} %fusion.406, f32[15,32,512]{2,1,0:T(8,128)S(1)} %collective-permute-done.17, f32[15,32,512]{2,1,0:T(8,128)S(1)} %collective-permute-done.16, f32[]{:T(128)} %bitcast.181, f32[]{:T(128)} %bitcast.180, f32[]{:T(128)} %bitcast.179, f32[]{:T(128)} %bitcast.178, ...), kind=kLoop, calls=%fused_computation.1493 | loop fusion | flops 23855104 | bytes 4063356 | tf_op jit(solution)/shard_map/add | solution.py:32
  453.7 14.3 %fusion.435 = f32[16,32,512]{2,1,0:T(8,128)S(1)} fusion(f32[16,32,512]{2,1,0:T(8,128)S(1)} %fusion.117, f32[4,16,32,512]{3,2,1,0:T(8,128)} %param.8, s32[]{:T(128)S(6)} %select_n.91, f32[]{:T(128)} %bitcast.209, f32[]{:T(128)} %bitcast.208, f32[]{:T(128)} %bitcast.207, f32[]{:T(128)} %bitcast.206, f32[]{:T(128)} %bitcast.205, f32[]{:T(128)} %bitcast.204, ...), kind=kLoop, calls=%fused_computation.1131 | loop fusion | flops 7864320 | bytes 3145792 | tf_op jit(solution)/shard_map/div | solution.py:57
  476.9 19.6 %collective-permute-done.21 = f32[15,32,512]{2,1,0:T(8,128)S(1)} collective-permute-done((f32[15,32,512]{2,1,0:T(8,128)S(1)}, f32[15,32,512]{2,1,0:T(8,128)S(1)}, u32[]{:S(2)}, u32[]{:S(2)}) %collective-permute-start.21) | collective-permute-done | bytes 983072 | tf_op jit(solution)/shard_map/ppermute | solution.py:14
  498.7 23.5 %fusion.711 = f32[16,32,512]{2,1,0:T(8,128)S(1)} fusion(f32[16,32,512]{2,1,0:T(8,128)S(1)} %fusion.435, f32[15,32,512]{2,1,0:T(8,128)S(1)} %collective-permute-done.21, f32[15,32,512]{2,1,0:T(8,128)S(1)} %collective-permute-done.20, f32[]{:T(128)} %bitcast.181, f32[]{:T(128)} %bitcast.180, f32[]{:T(128)} %bitcast.179, f32[]{:T(128)} %bitcast.178, ...), kind=kLoop, calls=%fused_computation.1407 | loop fusion | flops 23855104 | bytes 4063356 | tf_op jit(solution)/shard_map/add | solution.py:32
  535.0 11.9 %fusion.79 = f32[16,32,512]{2,1,0:T(8,128)S(1)} fusion(f32[16,32,512]{2,1,0:T(8,128)S(1)} %fusion.711, f32[16,7,512]{2,1,0:T(8,128)S(1)} %collective-permute-done.23, f32[16,7,512]{2,1,0:T(8,128)S(1)} %collective-permute-done.22, f32[]{:T(128)} %bitcast.195, f32[]{:T(128)} %bitcast.194, f32[]{:T(128)} %bitcast.193, f32[]{:T(128)} %bitcast.192, ...), kind=kLoop, calls=%fused_computation.775 | loop fusion | flops 11272192 | bytes 2555964 | tf_op jit(solution)/shard_map/add | solution.py:32
  546.9 13.2 %fusion.464 = f32[16,32,512]{2,1,0:T(8,128)S(1)} fusion(f32[16,32,512]{2,1,0:T(8,128)S(1)} %fusion.406, f32[16,32,512]{2,1,0:T(8,128)S(1)} %fusion.79, f32[]{:T(128)} %bitcast.209, f32[]{:T(128)} %bitcast.208, f32[]{:T(128)} %bitcast.207, f32[]{:T(128)} %bitcast.206, f32[]{:T(128)} %bitcast.205, f32[]{:T(128)} %bitcast.204, f32[]{:T(128)} %bitcast.203, ...), kind=kLoop, calls=%fused_computation.1160 | loop fusion | flops 7864320 | bytes 3145788 | tf_op jit(solution)/shard_map/mul | solution.py:58
  569.6 14.9 %collective-permute-done.25 = f32[15,32,512]{2,1,0:T(8,128)S(1)} collective-permute-done((f32[15,32,512]{2,1,0:T(8,128)S(1)}, f32[15,32,512]{2,1,0:T(8,128)S(1)}, u32[]{:S(2)}, u32[]{:S(2)}) %collective-permute-start.25) | collective-permute-done | bytes 983072 | tf_op jit(solution)/shard_map/ppermute | solution.py:15
  584.5 23.5 %fusion.625 = f32[16,32,512]{2,1,0:T(8,128)S(1)} fusion(f32[16,32,512]{2,1,0:T(8,128)S(1)} %fusion.464, f32[15,32,512]{2,1,0:T(8,128)S(1)} %collective-permute-done.25, f32[15,32,512]{2,1,0:T(8,128)S(1)} %collective-permute-done.24, f32[]{:T(128)} %bitcast.251, f32[]{:T(128)} %bitcast.250, f32[]{:T(128)} %bitcast.249, f32[]{:T(128)} %bitcast.248, ...), kind=kLoop, calls=%fused_computation.1321 | loop fusion | flops 23855104 | bytes 4063356 | tf_op jit(solution)/shard_map/add | solution.py:32
  637.5 14.3 %fusion.493 = f32[16,32,512]{2,1,0:T(8,128)S(1)} fusion(f32[16,32,512]{2,1,0:T(8,128)S(1)} %fusion.41, f32[4,16,32,512]{3,2,1,0:T(8,128)} %param.8, s32[]{:T(128)S(6)} %select_n.96, f32[]{:T(128)} %bitcast.279, f32[]{:T(128)} %bitcast.278, f32[]{:T(128)} %bitcast.277, f32[]{:T(128)} %bitcast.276, f32[]{:T(128)} %bitcast.275, f32[]{:T(128)} %bitcast.274, ...), kind=kLoop, calls=%fused_computation.1189 | loop fusion | flops 7864320 | bytes 3145792 | tf_op jit(solution)/shard_map/div | solution.py:57
  680.5 23.5 %fusion.539 = f32[16,32,512]{2,1,0:T(8,128)S(1)} fusion(f32[16,32,512]{2,1,0:T(8,128)S(1)} %fusion.493, f32[15,32,512]{2,1,0:T(8,128)S(1)} %collective-permute-done.29, f32[15,32,512]{2,1,0:T(8,128)S(1)} %collective-permute-done.28, f32[]{:T(128)} %bitcast.251, f32[]{:T(128)} %bitcast.250, f32[]{:T(128)} %bitcast.249, f32[]{:T(128)} %bitcast.248, ...), kind=kLoop, calls=%fused_computation.1235 | loop fusion | flops 23855104 | bytes 4063356 | tf_op jit(solution)/shard_map/add | solution.py:32
  718.9 11.9 %fusion.3 = f32[16,32,512]{2,1,0:T(8,128)S(1)} fusion(f32[16,32,512]{2,1,0:T(8,128)S(1)} %fusion.539, f32[16,7,512]{2,1,0:T(8,128)S(1)} %collective-permute-done.31, f32[16,7,512]{2,1,0:T(8,128)S(1)} %collective-permute-done.30, f32[]{:T(128)} %bitcast.265, f32[]{:T(128)} %bitcast.264, f32[]{:T(128)} %bitcast.263, f32[]{:T(128)} %bitcast.262, f32[]{:T(128)} %bitcast.261, ...), kind=kLoop, calls=%fused_computation.699 | loop fusion | flops 11272192 | bytes 2555964 | tf_op jit(solution)/shard_map/add | solution.py:32
  730.7 14.0 %fusion.522 = f32[16,32,512]{2,1,0:T(8,128)} fusion(f32[16,32,512]{2,1,0:T(8,128)S(1)} %fusion.464, f32[16,32,512]{2,1,0:T(8,128)S(1)} %fusion.3, f32[]{:T(128)} %bitcast.279, f32[]{:T(128)} %bitcast.278, f32[]{:T(128)} %bitcast.277, f32[]{:T(128)} %bitcast.276, f32[]{:T(128)} %bitcast.275, f32[]{:T(128)} %bitcast.274, f32[]{:T(128)} %bitcast.273, ...), kind=kLoop, calls=%fused_computation.1218 | loop fusion | flops 7864320 | bytes 3145788 | tf_op jit(solution)/shard_map/mul | solution.py:58
  (129 shorter events, 313.3 us)
Async XLA Ops:
  3.1 32.9 %collective-permute-start = (f32[15,32,512]{2,1,0:T(8,128)}, f32[15,32,512]{2,1,0:T(8,128)S(1)}, u32[]{:S(2)}, u32[]{:S(2)}) collective-permute-start(f32[15,32,512]{2,1,0:T(8,128)} %get-tuple-element.61), channel_id=1, source_target_pairs={{0,8},{8,16},{16,24},{24,32},{32,40},{40,48},{48,56},{56,64},{64,7... | collective-permute-start | bytes 2949128 | tf_op jit(solution)/shard_map/ppermute | solution.py:14
  5.2 31.3 %collective-permute-start.1 = (f32[15,32,512]{2,1,0:T(8,128)}, f32[15,32,512]{2,1,0:T(8,128)S(1)}, u32[]{:S(2)}, u32[]{:S(2)}) collective-permute-start(f32[15,32,512]{2,1,0:T(8,128)} %get-tuple-element.62), channel_id=1, source_target_pairs={{8,0},{16,8},{24,16},{32,24},{40,32},{48,40},{56,48},{64,56},{72,6... | collective-permute-start | bytes 2949128 | tf_op jit(solution)/shard_map/ppermute | solution.py:15
  60.0 11.5 %collective-permute-start.3 = (f32[16,7,512]{2,1,0:T(8,128)S(1)}, f32[16,7,512]{2,1,0:T(8,128)S(1)}, u32[]{:S(2)}, u32[]{:S(2)}) collective-permute-start(f32[16,7,512]{2,1,0:T(8,128)S(1)} %get-tuple-element.58), channel_id=1, source_target_pairs={{1,0},{2,1},{3,2},{4,3},{5,4},{6,5},{7,6},{9,8},{10,9},{11,10},{12... | collective-permute-start | bytes 688136 | tf_op jit(solution)/shard_map/ppermute | solution.py:15
  99.1 27.4 %collective-permute-start.5 = (f32[15,32,512]{2,1,0:T(8,128)S(1)}, f32[15,32,512]{2,1,0:T(8,128)S(1)}, u32[]{:S(2)}, u32[]{:S(2)}) collective-permute-start(f32[15,32,512]{2,1,0:T(8,128)S(1)} %get-tuple-element.56), channel_id=1, source_target_pairs={{0,8},{8,16},{16,24},{24,32},{32,40},{40,48},{48,56},{56,64},{64,7... | collective-permute-start | bytes 2949128 | tf_op jit(solution)/shard_map/ppermute | solution.py:14
  101.0 26.6 %collective-permute-start.4 = (f32[15,32,512]{2,1,0:T(8,128)S(1)}, f32[15,32,512]{2,1,0:T(8,128)S(1)}, u32[]{:S(2)}, u32[]{:S(2)}) collective-permute-start(f32[15,32,512]{2,1,0:T(8,128)S(1)} %get-tuple-element.55), channel_id=1, source_target_pairs={{8,0},{16,8},{24,16},{32,24},{40,32},{48,40},{56,48},{64,56},{72,6... | collective-permute-start | bytes 2949128 | tf_op jit(solution)/shard_map/ppermute | solution.py:15
  151.0 10.7 %collective-permute-start.7 = (f32[16,7,512]{2,1,0:T(8,128)S(1)}, f32[16,7,512]{2,1,0:T(8,128)S(1)}, u32[]{:S(2)}, u32[]{:S(2)}) collective-permute-start(f32[16,7,512]{2,1,0:T(8,128)S(1)} %get-tuple-element.54), channel_id=1, source_target_pairs={{0,1},{1,2},{2,3},{3,4},{4,5},{5,6},{6,7},{8,9},{9,10},{10,11},{11... | collective-permute-start | bytes 688136 | tf_op jit(solution)/shard_map/ppermute | solution.py:14
  152.9 12.2 %collective-permute-start.6 = (f32[16,7,512]{2,1,0:T(8,128)S(1)}, f32[16,7,512]{2,1,0:T(8,128)S(1)}, u32[]{:S(2)}, u32[]{:S(2)}) collective-permute-start(f32[16,7,512]{2,1,0:T(8,128)S(1)} %get-tuple-element.53), channel_id=1, source_target_pairs={{1,0},{2,1},{3,2},{4,3},{5,4},{6,5},{7,6},{9,8},{10,9},{11,10},{12... | collective-permute-start | bytes 688136 | tf_op jit(solution)/shard_map/ppermute | solution.py:15
  190.5 17.9 %collective-permute-start.9 = (f32[15,32,512]{2,1,0:T(8,128)S(1)}, f32[15,32,512]{2,1,0:T(8,128)S(1)}, u32[]{:S(2)}, u32[]{:S(2)}) collective-permute-start(f32[15,32,512]{2,1,0:T(8,128)S(1)} %get-tuple-element.52), channel_id=1, source_target_pairs={{8,0},{16,8},{24,16},{32,24},{40,32},{48,40},{56,48},{64,56},{72,6... | collective-permute-start | bytes 2949128 | tf_op jit(solution)/shard_map/ppermute | solution.py:15
  196.2 21.8 %collective-permute-start.8 = (f32[15,32,512]{2,1,0:T(8,128)S(1)}, f32[15,32,512]{2,1,0:T(8,128)S(1)}, u32[]{:S(2)}, u32[]{:S(2)}) collective-permute-start(f32[15,32,512]{2,1,0:T(8,128)S(1)} %get-tuple-element.51), channel_id=1, source_target_pairs={{0,8},{8,16},{16,24},{24,32},{32,40},{40,48},{48,56},{56,64},{64,7... | collective-permute-start | bytes 2949128 | tf_op jit(solution)/shard_map/ppermute | solution.py:14
  241.6 11.4 %collective-permute-start.11 = (f32[16,7,512]{2,1,0:T(8,128)S(1)}, f32[16,7,512]{2,1,0:T(8,128)S(1)}, u32[]{:S(2)}, u32[]{:S(2)}) collective-permute-start(f32[16,7,512]{2,1,0:T(8,128)S(1)} %get-tuple-element.50), channel_id=1, source_target_pairs={{1,0},{2,1},{3,2},{4,3},{5,4},{6,5},{7,6},{9,8},{10,9},{11,10},{12... | collective-permute-start | bytes 688136 | tf_op jit(solution)/shard_map/ppermute | solution.py:15
  283.7 27.5 %collective-permute-start.13 = (f32[15,32,512]{2,1,0:T(8,128)S(1)}, f32[15,32,512]{2,1,0:T(8,128)S(1)}, u32[]{:S(2)}, u32[]{:S(2)}) collective-permute-start(f32[15,32,512]{2,1,0:T(8,128)S(1)} %get-tuple-element.48), channel_id=1, source_target_pairs={{0,8},{8,16},{16,24},{24,32},{32,40},{40,48},{48,56},{56,64},{64,7... | collective-permute-start | bytes 2949128 | tf_op jit(solution)/shard_map/ppermute | solution.py:14
  285.6 28.7 %collective-permute-start.12 = (f32[15,32,512]{2,1,0:T(8,128)S(1)}, f32[15,32,512]{2,1,0:T(8,128)S(1)}, u32[]{:S(2)}, u32[]{:S(2)}) collective-permute-start(f32[15,32,512]{2,1,0:T(8,128)S(1)} %get-tuple-element.47), channel_id=1, source_target_pairs={{8,0},{16,8},{24,16},{32,24},{40,32},{48,40},{56,48},{64,56},{72,6... | collective-permute-start | bytes 2949128 | tf_op jit(solution)/shard_map/ppermute | solution.py:15
  339.8 10.4 %collective-permute-start.14 = (f32[16,7,512]{2,1,0:T(8,128)S(1)}, f32[16,7,512]{2,1,0:T(8,128)S(1)}, u32[]{:S(2)}, u32[]{:S(2)}) collective-permute-start(f32[16,7,512]{2,1,0:T(8,128)S(1)} %get-tuple-element.45), channel_id=1, source_target_pairs={{1,0},{2,1},{3,2},{4,3},{5,4},{6,5},{7,6},{9,8},{10,9},{11,10},{12... | collective-permute-start | bytes 688136 | tf_op jit(solution)/shard_map/ppermute | solution.py:15
  375.5 27.3 %collective-permute-start.17 = (f32[15,32,512]{2,1,0:T(8,128)S(1)}, f32[15,32,512]{2,1,0:T(8,128)S(1)}, u32[]{:S(2)}, u32[]{:S(2)}) collective-permute-start(f32[15,32,512]{2,1,0:T(8,128)S(1)} %get-tuple-element.44), channel_id=1, source_target_pairs={{8,0},{16,8},{24,16},{32,24},{40,32},{48,40},{56,48},{64,56},{72,6... | collective-permute-start | bytes 2949128 | tf_op jit(solution)/shard_map/ppermute | solution.py:15
  381.2 25.2 %collective-permute-start.16 = (f32[15,32,512]{2,1,0:T(8,128)S(1)}, f32[15,32,512]{2,1,0:T(8,128)S(1)}, u32[]{:S(2)}, u32[]{:S(2)}) collective-permute-start(f32[15,32,512]{2,1,0:T(8,128)S(1)} %get-tuple-element.43), channel_id=1, source_target_pairs={{0,8},{8,16},{16,24},{24,32},{32,40},{40,48},{48,56},{56,64},{64,7... | collective-permute-start | bytes 2949128 | tf_op jit(solution)/shard_map/ppermute | solution.py:14
  430.0 10.4 %collective-permute-start.19 = (f32[16,7,512]{2,1,0:T(8,128)S(1)}, f32[16,7,512]{2,1,0:T(8,128)S(1)}, u32[]{:S(2)}, u32[]{:S(2)}) collective-permute-start(f32[16,7,512]{2,1,0:T(8,128)S(1)} %get-tuple-element.42), channel_id=1, source_target_pairs={{1,0},{2,1},{3,2},{4,3},{5,4},{6,5},{7,6},{9,8},{10,9},{11,10},{12... | collective-permute-start | bytes 688136 | tf_op jit(solution)/shard_map/ppermute | solution.py:15
  468.3 28.2 %collective-permute-start.21 = (f32[15,32,512]{2,1,0:T(8,128)S(1)}, f32[15,32,512]{2,1,0:T(8,128)S(1)}, u32[]{:S(2)}, u32[]{:S(2)}) collective-permute-start(f32[15,32,512]{2,1,0:T(8,128)S(1)} %get-tuple-element.40), channel_id=1, source_target_pairs={{0,8},{8,16},{16,24},{24,32},{32,40},{40,48},{48,56},{56,64},{64,7... | collective-permute-start | bytes 2949128 | tf_op jit(solution)/shard_map/ppermute | solution.py:14
  470.2 28.5 %collective-permute-start.20 = (f32[15,32,512]{2,1,0:T(8,128)S(1)}, f32[15,32,512]{2,1,0:T(8,128)S(1)}, u32[]{:S(2)}, u32[]{:S(2)}) collective-permute-start(f32[15,32,512]{2,1,0:T(8,128)S(1)} %get-tuple-element.39), channel_id=1, source_target_pairs={{8,0},{16,8},{24,16},{32,24},{40,32},{48,40},{56,48},{64,56},{72,6... | collective-permute-start | bytes 2949128 | tf_op jit(solution)/shard_map/ppermute | solution.py:15
  560.5 24.0 %collective-permute-start.25 = (f32[15,32,512]{2,1,0:T(8,128)S(1)}, f32[15,32,512]{2,1,0:T(8,128)S(1)}, u32[]{:S(2)}, u32[]{:S(2)}) collective-permute-start(f32[15,32,512]{2,1,0:T(8,128)S(1)} %get-tuple-element.36), channel_id=1, source_target_pairs={{8,0},{16,8},{24,16},{32,24},{40,32},{48,40},{56,48},{64,56},{72,6... | collective-permute-start | bytes 2949128 | tf_op jit(solution)/shard_map/ppermute | solution.py:15
  565.6 18.9 %collective-permute-start.24 = (f32[15,32,512]{2,1,0:T(8,128)S(1)}, f32[15,32,512]{2,1,0:T(8,128)S(1)}, u32[]{:S(2)}, u32[]{:S(2)}) collective-permute-start(f32[15,32,512]{2,1,0:T(8,128)S(1)} %get-tuple-element.35), channel_id=1, source_target_pairs={{0,8},{8,16},{16,24},{24,32},{32,40},{40,48},{48,56},{56,64},{64,7... | collective-permute-start | bytes 2949128 | tf_op jit(solution)/shard_map/ppermute | solution.py:14
  608.1 16.1 %collective-permute-start.27 = (f32[16,7,512]{2,1,0:T(8,128)S(1)}, f32[16,7,512]{2,1,0:T(8,128)S(1)}, u32[]{:S(2)}, u32[]{:S(2)}) collective-permute-start(f32[16,7,512]{2,1,0:T(8,128)S(1)} %get-tuple-element.34), channel_id=1, source_target_pairs={{1,0},{2,1},{3,2},{4,3},{5,4},{6,5},{7,6},{9,8},{10,9},{11,10},{12... | collective-permute-start | bytes 688136 | tf_op jit(solution)/shard_map/ppermute | solution.py:15
  614.4 11.2 %collective-permute-start.26 = (f32[16,7,512]{2,1,0:T(8,128)S(1)}, f32[16,7,512]{2,1,0:T(8,128)S(1)}, u32[]{:S(2)}, u32[]{:S(2)}) collective-permute-start(f32[16,7,512]{2,1,0:T(8,128)S(1)} %get-tuple-element.33), channel_id=1, source_target_pairs={{0,1},{1,2},{2,3},{3,4},{4,5},{5,6},{6,7},{8,9},{9,10},{10,11},{11... | collective-permute-start | bytes 688136 | tf_op jit(solution)/shard_map/ppermute | solution.py:14
  652.0 20.3 %collective-permute-start.29 = (f32[15,32,512]{2,1,0:T(8,128)S(1)}, f32[15,32,512]{2,1,0:T(8,128)S(1)}, u32[]{:S(2)}, u32[]{:S(2)}) collective-permute-start(f32[15,32,512]{2,1,0:T(8,128)S(1)} %get-tuple-element.32), channel_id=1, source_target_pairs={{0,8},{8,16},{16,24},{24,32},{32,40},{40,48},{48,56},{56,64},{64,7... | collective-permute-start | bytes 2949128 | tf_op jit(solution)/shard_map/ppermute | solution.py:14
  653.9 26.6 %collective-permute-start.28 = (f32[15,32,512]{2,1,0:T(8,128)S(1)}, f32[15,32,512]{2,1,0:T(8,128)S(1)}, u32[]{:S(2)}, u32[]{:S(2)}) collective-permute-start(f32[15,32,512]{2,1,0:T(8,128)S(1)} %get-tuple-element.31), channel_id=1, source_target_pairs={{8,0},{16,8},{24,16},{32,24},{40,32},{48,40},{56,48},{64,56},{72,6... | collective-permute-start | bytes 2949128 | tf_op jit(solution)/shard_map/ppermute | solution.py:15
  (14 other events, 216.1 us)
where the time goes:
time: 757 us; the launch traced here: 745 us
  other arithmetic  410 us (54%)
  waiting for transfers between devices  176 us (23%)
  starting transfers between devices  130 us (17%)
  local copies, waits for them, and re-layouts  19.9 us (3%)
  between operations  8.36 us (1%)
    add x16, other arithmetic, correlate_padded(): total = term if total is None else total + term  283 us
    ppermute x16, waiting for transfers between devices, with_halo(): before = lax.ppermute(last, axis, up)  101 us
    ppermute x16, starting transfers between devices, with_halo(): after = lax.ppermute(initial, axis, down)  85.2 us
    ppermute x16, waiting for transfers between devices, with_halo(): after = lax.ppermute(initial, axis, down)  74.8 us
    div x4, other arithmetic, on_device(): ratio = recorded / blurred  57.4 us
    mul x4, other arithmetic, on_device(): current = current * blur(ratio, weights_z, weights_y, weights_x, True)  53.8 us
    ppermute x16, starting transfers between devices, with_halo(): before = lax.ppermute(last, axis, up)  45 us
  transfers between devices with their start and end apart: 32, of which 28 were waited for; matrix products, arithmetic and copies ran while one was open for 4% of the time, Pallas kernels for 0%

commit v1 on v0

v1 whole, which is shorter than its diff:
```python
import functools

import jax
import jax.numpy as jnp
from jax import lax
from jax.experimental import pallas as pl
from jax.experimental.pallas import tpu as pltpu
from jax.sharding import PartitionSpec as P


REACH_Z = 15
REACH_L = 7
TAPS_Z = 2 * REACH_Z + 1
TAPS_L = 2 * REACH_L + 1
REACHES = (7, 11, 15)
F32 = jnp.float32
BF16 = jnp.bfloat16

VMEM_SPEC = pl.BlockSpec(memory_space=pltpu.VMEM)
SMEM_SPEC = pl.BlockSpec(memory_space=pltpu.SMEM)
ANY_SPEC = pl.BlockSpec(memory_space=pl.ANY)


def params(mib):
    return pltpu.CompilerParams(vmem_limit_bytes=mib << 20)


def cost(flops, moved):
    return pl.CostEstimate(flops=flops, bytes_accessed=moved, transcendentals=0)


def halves(x):
    hi = x.astype(BF16)
    return hi, (x - hi.astype(F32)).astype(BF16)


def mm(a, b):
    return jnp.dot(a, b, preferred_element_type=F32)


def stacked(w, x):
    hi, lo = halves(x)
    tall = w.shape[0] // 2
    both = mm(w, hi)
    return both[:tall] + both[tall:] + mm(w[:tall], lo)


def iota2(shape, dim):
    return lax.broadcasted_iota(jnp.int32, shape, dim)


def tap_table(psf_ref, extents_ref, order_ref, pos, flip, axis, count):
    view = order_ref[pos]
    radius = (extents_ref[view, axis] - 1) // 2
    reach = count // 2
    kept = []
    for k in range(count):
        source = jnp.where(flip == 1, count - 1 - k, k)
        kept.append(jnp.where(abs(k - reach) <= radius, psf_ref[view, source], 0.0))
    total = kept[0]
    for tap in kept[1:]:
        total = total + tap
    return kept, total


def banded(place, table):
    kept, total = table
    value = jnp.zeros(place.shape, F32)
    for k, tap in enumerate(kept):
        value = jnp.where(place == k, tap, value)
    return halves(value / jnp.full(place.shape, total, F32))


def middle_bands(table, odd):
    first = jnp.where(odd == 1, 0, 24)
    last = 24 - first
    r = iota2((128, 256), 0)
    c = iota2((128, 256), 1)
    q = c & 31
    yi = jnp.where(q < 8, q + first, jnp.where(q < 24, q, q - 24 + last))
    return banded(jnp.where((r >> 4) == (c >> 5), yi - ((r & 15) + 8) + REACH_L, -1), table)


def edge_bands(table, odd):
    first = jnp.where(odd == 1, 0, 24)
    last = 24 - first
    outer_first = jnp.where(odd == 1, -8, 32)
    outer_last = 24 - outer_first
    r = iota2((64, 192), 0)
    c = iota2((64, 192), 1)
    zc = jnp.where(c >= 144, 3, jnp.where(c >= 96, 2, jnp.where(c >= 48, 1, 0)))
    q = c - 48 * zc
    e = r & 15
    yo = jnp.where(e < 8, e + first, e - 8 + last)
    yi = jnp.where(
        q < 8,
        q + outer_first,
        jnp.where(q < 16, q - 8 + first, jnp.where(q < 32, q - 8, jnp.where(q < 40, q - 32 + last, q - 40 + outer_last))),
    )
    return banded(jnp.where((r >> 4) == zc, yi - yo + REACH_L, -1), table)


def prepare_kernel(planes, pos_ref, order_ref, extents_ref, psf_z_ref, psf_y_ref, psf_x_ref, par_ref, ye_ref, ym_ref, z_ref, x_ref):
    par = par_ref[0]
    pos = pos_ref[0]
    tall = 8 * planes
    wide = z_ref.shape[-1]
    blocks = x_ref.shape[-1] // 128

    def one(flip, carry):
        table = tap_table(psf_y_ref, extents_ref, order_ref, pos, flip, 1, TAPS_L)
        hi, lo = edge_bands(table, par_ref[1])
        ye_ref[flip, :64, :] = hi
        ye_ref[flip, 64:, :] = lo
        hi, lo = middle_bands(table, par_ref[1])
        ym_ref[flip, :128, :] = hi
        ym_ref[flip, 128:, :] = lo

        table = tap_table(psf_z_ref, extents_ref, order_ref, pos, flip, 0, TAPS_Z)

        def z_rows(chunk, inner):
            base = pl.multiple_of(chunk * 16, 16)
            r = iota2((16, wide), 0) + base
            c = iota2((16, wide), 1)
            plane = c >> 3
            second = plane >= 2 * planes
            j = jnp.where(second, plane - 2 * planes, plane - planes)
            below = jnp.where(second, 1 - par, par) == 1
            i = jnp.where(plane < planes, plane, jnp.where(below, -1 - j, planes + j))
            d = jnp.where((r & 7) == (c & 7), i - (r >> 3) + REACH_Z, -1)
            hi, lo = banded(d, table)
            z_ref[flip, pl.ds(base, 16), :] = hi
            z_ref[flip, pl.ds(tall + base, 16), :] = lo
            return inner

        lax.fori_loop(0, tall // 16, z_rows, 0)

        table = tap_table(psf_x_ref, extents_ref, order_ref, pos, flip, 2, TAPS_L)
        d = iota2((128, 128), 0) - iota2((128, 128), 1) + REACH_L
        for shift in (-1, 0, 1):
            hi, lo = banded(d + 128 * shift, table)
            for b in range(blocks):
                a = b + shift
                if 0 <= a < blocks:
                    x_ref[flip, 0, 128 * a:128 * a + 128, 128 * b:128 * b + 128] = hi
                    x_ref[flip, 1, 128 * a:128 * a + 128, 128 * b:128 * b + 128] = lo
        zero = jnp.zeros((128, 128), BF16)
        for a in range(blocks):
            for b in range(blocks):
                if abs(a - b) > 1:
                    x_ref[flip, 0, 128 * a:128 * a + 128, 128 * b:128 * b + 128] = zero
                    x_ref[flip, 1, 128 * a:128 * a + 128, 128 * b:128 * b + 128] = zero
        return carry

    lax.fori_loop(0, 2, one, 0)


def tall_rows(planes, *values):
    rows = []
    for v in values:
        rows.append(v.reshape(-1, v.shape[-1]))
        missing = 8 * (planes - v.shape[0])
        if missing:
            rows.append(jnp.zeros((missing, v.shape[-1]), F32))
    return jnp.concatenate(rows, axis=0)


def x_stage(w, rows):
    hi, lo = halves(rows)
    return mm(hi, w[0]) + mm(lo, w[0]) + mm(hi, w[1])


def inner_z(wz, own_ref, a_ref, out_ref):
    planes, half, width = out_ref.shape
    split = 16 * planes
    for g in range(0, half, 8):
        x = tall_rows(planes, own_ref[:, g:g + 8, :], a_ref[:, g:g + 8, :])
        out_ref[:, g:g + 8, :] = stacked(wz[:, :split], x).reshape(planes, 8, width)


def outer_zx(wz, wx, inner_ref, b_ref, z_buf):
    planes, half, width = z_buf.shape
    split = 16 * planes
    for g in range(0, half, 8):
        x = tall_rows(planes, b_ref[:, g:g + 8, :])
        z_buf[:, g:g + 8, :] = inner_ref[:, g:g + 8, :] + stacked(wz[:, split:], x).reshape(planes, 8, width)
    return x_stage(wx, z_buf[...].reshape(planes * half, width)).reshape(z_buf.shape)


def zx_stage(wz, wx, own_ref, a_ref, b_ref, z_buf):
    planes, half, width = z_buf.shape
    for g in range(0, half, 8):
        x = tall_rows(planes, own_ref[:, g:g + 8, :], a_ref[:, g:g + 8, :], b_ref[:, g:g + 8, :])
        z_buf[:, g:g + 8, :] = stacked(wz, x).reshape(planes, 8, width)
    return x_stage(wx, z_buf[...].reshape(planes * half, width)).reshape(z_buf.shape)


def send_parts(par, whole_ref, a_ref, b_ref):
    last = whole_ref.shape[0] - 1

    def one(j, carry):
        b_ref[j] = whole_ref[jnp.where(par == 1, last - j, j)]
        a_ref[j] = whole_ref[jnp.where(par == 1, j, last - j)]
        return carry

    lax.fori_loop(0, a_ref.shape[0], one, 0)


def y_middle(w, e0_ref, m_ref, e1_ref, out_ref):
    for q in range(0, m_ref.shape[0], 8):
        pieces = []
        for z in range(q, q + 8):
            pieces += [r[z] for r in (e0_ref, m_ref, e1_ref)]
        out_ref[q:q + 8] = stacked(w, jnp.concatenate(pieces, axis=0)).reshape(8, 16, m_ref.shape[-1])


def edge_rows(odd):
    first = pl.multiple_of(jnp.where(odd == 1, 0, 24), 8)
    last = pl.multiple_of(jnp.where(odd == 1, 24, 0), 8)
    return pl.ds(first, 8), pl.ds(last, 8)


def split_kernel(par_ref, f_hbm, e0_ref, e1_ref, m_ref, sems):
    first, last = edge_rows(par_ref[1])
    copies = [
        pltpu.make_async_copy(f_hbm.at[:, rows, :], out, sems.at[i])
        for i, (rows, out) in enumerate(((first, e0_ref), (last, e1_ref), (pl.ds(8, 16), m_ref)))
    ]
    for copy in copies:
        copy.start()
    for copy in copies:
        copy.wait()


def merge_kernel(par_ref, e0_ref, e1_ref, m_ref, out_ref):
    first, last = edge_rows(par_ref[1])
    out_ref[:, first, :] = e0_ref[...]
    out_ref[:, last, :] = e1_ref[...]
    out_ref[:, 8:24, :] = m_ref[...]


def open_kernel(pos_ref, order_ref, extents_ref, psf_ref, par_ref, e0_ref, m_ref, e1_ref, ny_ref, na_ref, nb_ref, w_buf):
    hi, lo = middle_bands(tap_table(psf_ref, extents_ref, order_ref, pos_ref[0], 0, 1, TAPS_L), par_ref[1])
    w_buf[:128, :] = hi
    w_buf[128:, :] = lo
    y_middle(w_buf[...], e0_ref, m_ref, e1_ref, ny_ref)
    send_parts(par_ref[0], ny_ref, na_ref, nb_ref)


def edge_y_kernel(flip, par_ref, ye_ref, e0_ref, m_ref, e1_ref, r0_ref, r1_ref, ny_ref, na_ref, nb_ref):
    for q in range(0, m_ref.shape[0], 4):
        pieces = []
        for z in range(q, q + 4):
            pieces += [r[z] for r in (r0_ref, e0_ref, m_ref, e1_ref, r1_ref)]
        ny_ref[q:q + 4] = stacked(ye_ref[flip], jnp.concatenate(pieces, axis=0)).reshape(4, 16, m_ref.shape[-1])
    send_parts(par_ref[0], ny_ref, na_ref, nb_ref)


def inner_kernel(flip, wz_ref, own_ref, a_ref, out_ref):
    inner_z(wz_ref[flip], own_ref, a_ref, out_ref)


def middle_kernel(flip, pos_ref, order_ref, wz_ref, wx_ref, own_ref, a_ref, b_ref, other_ref, m_ref, z_buf, m_buf, sem):
    if flip == 0:
        copy = pltpu.make_async_copy(other_ref.at[order_ref[pos_ref[0]], :, 8:24, :], m_buf, sem.at[0])
        copy.start()
    result = zx_stage(wz_ref[flip], wx_ref.at[flip], own_ref, a_ref, b_ref, z_buf)
    if flip == 0:
        copy.wait()
        m_ref[...] = m_buf[...] / result
    else:
        m_ref[...] = other_ref[...] * result


def forward_edge_kernel(par_ref, pos_ref, order_ref, wz_ref, wx_ref, ym_ref, inner_ref, b_ref, m_ref, measured_ref,
                        e0_ref, e1_ref, ny_ref, na_ref, nb_ref, z_buf, m_buf, sems):
    first, last = edge_rows(par_ref[1])
    view = order_ref[pos_ref[0]]
    copies = [
        pltpu.make_async_copy(measured_ref.at[view, :, rows, :], m_buf.at[:, 8 * i:8 * i + 8, :], sems.at[i])
        for i, rows in enumerate((first, last))
    ]
    for copy in copies:
        copy.start()
    result = outer_zx(wz_ref[0], wx_ref.at[0], inner_ref, b_ref, z_buf)
    for copy in copies:
        copy.wait()
    e0_ref[...] = m_buf[:, :8, :] / result[:, :8]
    e1_ref[...] = m_buf[:, 8:, :] / result[:, 8:]
    y_middle(ym_ref[1], e0_ref, m_ref, e1_ref, ny_ref)
    send_parts(par_ref[0], ny_ref, na_ref, nb_ref)


def adjoint_edge_kernel(wz_ref, wx_ref, inner_ref, b_ref, other0_ref, other1_ref, e0_ref, e1_ref, z_buf):
    result = outer_zx(wz_ref[1], wx_ref.at[1], inner_ref, b_ref, z_buf)
    e0_ref[...] = other0_ref[...] * result[:, :8]
    e1_ref[...] = other1_ref[...] * result[:, 8:]


def pair_exchange(value, axis, odd):
    size = lax.axis_size(axis)
    pairs = [(i, i + 1) for i in range(odd, size - 1, 2)]
    return lax.ppermute(value, axis, pairs + [(j, i) for i, j in pairs])


def call(kernel, ins, outs, flops, scratch=(), mib=12):
    return pl.pallas_call(
        kernel,
        in_specs=ins,
        out_specs=[VMEM_SPEC] * len(outs),
        out_shape=outs,
        scratch_shapes=list(scratch),
        compiler_params=params(mib),
        cost_estimate=cost(flops, 4_000_000),
    )


def view_pass(reach, shapes, parity, tables, measured, pos, e0, e1, m):
    group, half = shapes
    planes, _, width = half.shape
    order, extents, psf_z, psf_y, psf_x = tables
    part = jax.ShapeDtypeStruct((reach, 16, width), F32)
    dma = pltpu.SemaphoreType.DMA
    z_buf = pltpu.VMEM(half.shape, F32)
    m_buf = pltpu.VMEM(half.shape, F32)
    sm, vm = SMEM_SPEC, VMEM_SPEC

    ny, na, nb = call(open_kernel, [sm] * 5 + [vm] * 3, [half, part, part], 200_000_000,
                      [pltpu.VMEM((256, 256), BF16)])(pos, order, extents, psf_y, parity, e0, m, e1)
    weights = [jax.ShapeDtypeStruct((2,) + s, BF16)
               for s in ((128, 192), (256, 256), (16 * planes, 24 * planes), (2, width, width))]
    mye, mym, mz, mx = call(functools.partial(prepare_kernel, planes), [sm] * 7, weights, 20_000_000, mib=8)(
        pos, order, extents, psf_z, psf_y, psf_x, parity)
    current = (e0, e1, m)
    for flip in (0, 1):
        r1 = pair_exchange(e1, "gy", 1)
        bm = pair_exchange(nb, "gz", 1)
        r0 = pair_exchange(e0, "gy", 0)
        am = pair_exchange(na, "gz", 0)
        ey, ea, eb = call(functools.partial(edge_y_kernel, flip), [sm] + [vm] * 6, [half, part, part],
                          400_000_000)(parity, mye, e0, m, e1, r0, r1)
        be = pair_exchange(eb, "gz", 1)
        ae = pair_exchange(ea, "gz", 0)
        m, = call(functools.partial(middle_kernel, flip), [sm] * 2 + [vm] * 5 + [vm if flip else ANY_SPEC],
                  [half], 1_000_000_000, [z_buf, m_buf, dma((1,))])(
            pos, order, mz, mx, ny, am, bm, current[2] if flip else measured)
        inner, = call(functools.partial(inner_kernel, flip), [vm] * 3, [half], 400_000_000)(mz, ey, ae)
        if flip == 0:
            e0, e1, ny, na, nb = call(forward_edge_kernel, [sm] * 3 + [vm] * 6 + [ANY_SPEC],
                                      [group, group, half, part, part], 1_200_000_000, [z_buf, m_buf, dma((2,))])(
                parity, pos, order, mz, mx, mym, inner, be, m, measured)
        else:
            e0, e1 = call(adjoint_edge_kernel, [vm] * 6, [group, group], 1_000_000_000, [z_buf])(
                mz, mx, inner, be, current[0], current[1])
    return e0, e1, m


def on_device(estimate, measured, psf_z, psf_y, psf_x, extents, order):
    planes, _, width = estimate.shape
    views = measured.shape[0]
    reaches = tuple(min(r, planes) for r in REACHES)
    parity = jnp.stack([lax.axis_index("gz") & 1, lax.axis_index("gy") & 1]).astype(jnp.int32)
    half = jax.ShapeDtypeStruct((planes, 16, width), F32)
    group = jax.ShapeDtypeStruct((planes, 8, width), F32)
    whole = jax.ShapeDtypeStruct(estimate.shape, F32)
    tables = (order, extents, psf_z, psf_y, psf_x)
    radii = (extents[:, 0] - 1) // 2
    sizes = sum((radii > r).astype(jnp.int32) for r in REACHES[:-1]) if len(REACHES) > 1 else jnp.zeros_like(radii)

    state = call(split_kernel, [SMEM_SPEC, ANY_SPEC], [group, group, half], 1, [pltpu.SemaphoreType.DMA((3,))])(
        parity, estimate)
    passes = [functools.partial(view_pass, r, (group, half), parity, tables, measured) for r in reaches]
    packed = jnp.sum(sizes[order] << (2 * jnp.arange(views, dtype=jnp.int32)))

    def step(index, state):
        pos = jnp.reshape(index, (1,)).astype(jnp.int32)
        if len(passes) == 1:
            return (state[0],) + tuple(passes[0](pos, *state[1:]))
        return (state[0] >> 2,) + tuple(lax.switch(state[0] & 3, passes, pos, *state[1:]))

    state = lax.fori_loop(0, views, step, (packed, *state))[1:]
    return call(merge_kernel, [SMEM_SPEC] + [VMEM_SPEC] * 3, [whole], 1)(parity, *state)[0]


def solution(mesh):
    return jax.shard_map(
        on_device,
        mesh=mesh,
        in_specs=(P("gz", "gy", None), P(None, "gz", "gy", None), P(), P(), P(), P(), P()),
        out_specs=P("gz", "gy", None),
        check_vma=False,
    )
```

time: 757 us -> 299 us (0.39)
  the two profiles are of different devices: /device:TPU:30 before, /device:TPU:40 now
where the time goes in v1:
time: 299 us; the launch traced here: 298 us
  waiting for transfers between devices  134 us (45%)
  starting transfers between devices  92.4 us (31%)
  Pallas kernels  60.4 us (20%)
  loops' own time  7.51 us (3%)
    ppermute x48, waiting for transfers between devices, pair_exchange(): return lax.ppermute(value, axis, pairs + [(j, i) for i, j in pairs])  134 us
    ppermute x48, starting transfers between devices, pair_exchange(): return lax.ppermute(value, axis, pairs + [(j, i) for i, j in pairs])  92.4 us
    pallas_call x8, Pallas kernels, view_pass(): call(functools.partial(middle_kernel, flip), [sm] * 2 + [vm] * 5 + [vm if...  15.9 us
    pallas_call x4, Pallas kernels, view_pass(): call(functools.partial(prepare_kernel, planes), [sm] * 7, weights, 200000...  13.3 us
    pallas_call x8, Pallas kernels, view_pass(): call(functools.partial(edge_y_kernel, flip), [sm] + [vm] * 6, [half, part...  8.74 us
    pallas_call x4, Pallas kernels, view_pass(): call(forward_edge_kernel, [sm] * 3 + [vm] * 6 + [ANY_SPEC], [group, group...  8.07 us
    another operation x1, loops' own time, on_device(): state = lax.fori_loop(0, views, step, (packed, *state))[1:]  6.47 us
  transfers between devices with their start and end apart: 48, of which 18 were waited for; matrix products, arithmetic and copies ran while one was open for 0% of the time, Pallas kernels for 16%

profile of v1, /device:TPU:40, one launch (start us, length us, event | category | flops | bytes accessed | tf_op | source)
XLA Modules:
  0.0 298.3 jit_solution(10013100346723467297)
XLA Ops:
  4.7 292.0 %while.19 = (s32[]{:T(128)}, s32[]{:T(128)}, f32[16,8,512]{2,1,0:T(8,128)S(1)}, f32[16,8,512]{2,1,0:T(8,128)S(1)}, f32[16,16,512]{2,1,0:T(8,128)S(1)}, /*index=5...) while((s32[]{:T(128)}, s32[]{:T(128)}, ...), condition=%wide.region_5.6_spmd, body=%wide.region_1.5_spmd.sunk | while | flops 6020000256 | bytes 78798216 | solution.py:381
  5.2 74.2 %conditional.2 = (f32[16,8,512]{2,1,0:T(8,128)S(1)}, f32[16,8,512]{2,1,0:T(8,128)S(1)}, f32[16,16,512]{2,1,0:T(8,128)S(1)}) conditional(s32[]{:T(128)} %clamp.10, (s32[1]{0:T(128)}, s32[4]{0:T(128)}, s32[4,3]{1,0:T(4,128)}, f32[4,31]{1,0:T(4,128)}, f32[4,15]{1,0:T(4,128)}, /*index=5*/f32[4,15]{1,0:T(4,128)}, s32[2]{0:T(128)S(1)}, ...), branch_computations={%region_2.2_spmd, %region_3.3_spmd, %region_4.4_spmd} | conditional | flops 6020000256 | bytes 76700784 | solution.py:379
  11.9 8.2 %collective-permute-start.29 = (f32[15,16,512]{2,1,0:T(8,128)S(1)}, f32[15,16,512]{2,1,0:T(8,128)S(1)}, u32[]{:S(2)}, u32[]{:S(2)}) collective-permute-start(f32[15,16,512]{2,1,0:T(8,128)S(1)} %get-tuple-element.343), channel_id=1, source_target_pairs={{8,16},{24,32},{40,48},{56,64},{72,80},{88,96},{104,112},{120,128}... | collective-permute-start | bytes 1474568 | tf_op jit(solution)/shard_map/while/body/eval_jaxpr/cond/branch_2_fun/ppermute | solution.py:303
  24.7 9.9 %collective-permute-start.27 = (f32[15,16,512]{2,1,0:T(8,128)S(1)}, f32[15,16,512]{2,1,0:T(8,128)S(1)}, u32[]{:S(2)}, u32[]{:S(2)}) collective-permute-start(f32[15,16,512]{2,1,0:T(8,128)S(1)} %get-tuple-element.340), channel_id=1, source_target_pairs={{8,16},{24,32},{40,48},{56,64},{72,80},{88,96},{104,112},{120,128}... | collective-permute-start | bytes 1474568 | tf_op jit(solution)/shard_map/while/body/eval_jaxpr/cond/branch_2_fun/ppermute | solution.py:303
  43.3 5.8 %collective-permute-start.31 = (f32[16,8,512]{2,1,0:T(8,128)S(1)}, f32[16,8,512]{2,1,0:T(8,128)S(1)}, u32[]{:S(2)}, u32[]{:S(2)}) collective-permute-start(f32[16,8,512]{2,1,0:T(8,128)S(1)} %get-tuple-element.346.e1_ref), channel_id=1, source_target_pairs={{1,2},{3,4},{5,6},{2,1},{4,3},{6,5},{9,10},{11,12},{13,14},{10,9},... | collective-permute-start | bytes 786440 | tf_op jit(solution)/shard_map/while/body/eval_jaxpr/cond/branch_2_fun/ppermute | solution.py:303
  53.9 10.0 %collective-permute-done.31.r1_ref = f32[16,8,512]{2,1,0:T(8,128)S(1)} collective-permute-done((f32[16,8,512]{2,1,0:T(8,128)S(1)}, f32[16,8,512]{2,1,0:T(8,128)S(1)}, u32[]{:S(2)}, u32[]{:S(2)}) %collective-permute-start.31) | collective-permute-done | bytes 262176 | tf_op jit(solution)/shard_map/while/body/eval_jaxpr/cond/branch_2_fun/ppermute | solution.py:303
  65.1 6.9 %collective-permute-start.33 = (f32[15,16,512]{2,1,0:T(8,128)S(1)}, f32[15,16,512]{2,1,0:T(8,128)S(1)}, u32[]{:S(2)}, u32[]{:S(2)}) collective-permute-start(f32[15,16,512]{2,1,0:T(8,128)S(1)} %get-tuple-element.349), channel_id=1, source_target_pairs={{8,16},{24,32},{40,48},{56,64},{72,80},{88,96},{104,112},{120,128}... | collective-permute-start | bytes 1474568 | tf_op jit(solution)/shard_map/while/body/eval_jaxpr/cond/branch_2_fun/ppermute | solution.py:303
  81.1 69.8 %conditional.2 = (f32[16,8,512]{2,1,0:T(8,128)S(1)}, f32[16,8,512]{2,1,0:T(8,128)S(1)}, f32[16,16,512]{2,1,0:T(8,128)S(1)}) conditional(s32[]{:T(128)} %clamp.10, (s32[1]{0:T(128)}, s32[4]{0:T(128)}, s32[4,3]{1,0:T(4,128)}, f32[4,31]{1,0:T(4,128)}, f32[4,15]{1,0:T(4,128)}, /*index=5*/f32[4,15]{1,0:T(4,128)}, s32[2]{0:T(128)S(1)}, ...), branch_computations={%region_2.2_spmd, %region_3.3_spmd, %region_4.4_spmd} | conditional | flops 6020000256 | bytes 76700784 | solution.py:379
  82.8 4.7 %collective-permute-start.13 = (f32[16,8,512]{2,1,0:T(8,128)S(1)}, f32[16,8,512]{2,1,0:T(8,128)S(1)}, u32[]{:S(2)}, u32[]{:S(2)}) collective-permute-start(f32[16,8,512]{2,1,0:T(8,128)S(1)} %get-tuple-element.306.e1_ref.other1_ref), channel_id=1, source_target_pairs={{1,2},{3,4},{5,6},{2,1},{4,3},{6,5},{9,10},{11,12},{13,14},{10,9},... | collective-permute-start | bytes 786440 | tf_op jit(solution)/shard_map/while/body/eval_jaxpr/cond/branch_1_fun/ppermute | solution.py:303
  94.7 5.0 %collective-permute-done.13.r1_ref = f32[16,8,512]{2,1,0:T(8,128)S(1)} collective-permute-done((f32[16,8,512]{2,1,0:T(8,128)S(1)}, f32[16,8,512]{2,1,0:T(8,128)S(1)}, u32[]{:S(2)}, u32[]{:S(2)}) %collective-permute-start.13) | collective-permute-done | bytes 262176 | tf_op jit(solution)/shard_map/while/body/eval_jaxpr/cond/branch_1_fun/ppermute | solution.py:303
  107.3 5.3 %collective-permute-done.15.b_ref = f32[11,16,512]{2,1,0:T(8,128)S(1)} collective-permute-done((f32[11,16,512]{2,1,0:T(8,128)S(1)}, f32[11,16,512]{2,1,0:T(8,128)S(1)}, u32[]{:S(2)}, u32[]{:S(2)}) %collective-permute-start.15) | collective-permute-done | bytes 360480 | tf_op jit(solution)/shard_map/while/body/eval_jaxpr/cond/branch_1_fun/ppermute | solution.py:303
  118.5 6.0 %collective-permute-start.23 = (f32[11,16,512]{2,1,0:T(8,128)S(1)}, f32[11,16,512]{2,1,0:T(8,128)S(1)}, u32[]{:S(2)}, u32[]{:S(2)}) collective-permute-start(f32[11,16,512]{2,1,0:T(8,128)S(1)} %get-tuple-element.323), channel_id=1, source_target_pairs={{8,16},{24,32},{40,48},{56,64},{72,80},{88,96},{104,112},{120,128}... | collective-permute-start | bytes 1081352 | tf_op jit(solution)/shard_map/while/body/eval_jaxpr/cond/branch_1_fun/ppermute | solution.py:303
  124.5 12.6 %collective-permute-done.19.r1_ref = f32[16,8,512]{2,1,0:T(8,128)S(1)} collective-permute-done((f32[16,8,512]{2,1,0:T(8,128)S(1)}, f32[16,8,512]{2,1,0:T(8,128)S(1)}, u32[]{:S(2)}, u32[]{:S(2)}) %collective-permute-start.19) | collective-permute-done | bytes 262176 | tf_op jit(solution)/shard_map/while/body/eval_jaxpr/cond/branch_1_fun/ppermute | solution.py:303
  142.3 7.8 %collective-permute-done.21.b_ref = f32[11,16,512]{2,1,0:T(8,128)S(1)} collective-permute-done((f32[11,16,512]{2,1,0:T(8,128)S(1)}, f32[11,16,512]{2,1,0:T(8,128)S(1)}, u32[]{:S(2)}, u32[]{:S(2)}) %collective-permute-start.21) | collective-permute-done | bytes 360480 | tf_op jit(solution)/shard_map/while/body/eval_jaxpr/cond/branch_1_fun/ppermute | solution.py:303
  152.7 68.6 %conditional.2 = (f32[16,8,512]{2,1,0:T(8,128)S(1)}, f32[16,8,512]{2,1,0:T(8,128)S(1)}, f32[16,16,512]{2,1,0:T(8,128)S(1)}) conditional(s32[]{:T(128)} %clamp.10, (s32[1]{0:T(128)}, s32[4]{0:T(128)}, s32[4,3]{1,0:T(4,128)}, f32[4,31]{1,0:T(4,128)}, f32[4,15]{1,0:T(4,128)}, /*index=5*/f32[4,15]{1,0:T(4,128)}, s32[2]{0:T(128)S(1)}, ...), branch_computations={%region_2.2_spmd, %region_3.3_spmd, %region_4.4_spmd} | conditional | flops 6020000256 | bytes 76700784 | solution.py:379
  161.5 11.6 %collective-permute-done.13.r1_ref = f32[16,8,512]{2,1,0:T(8,128)S(1)} collective-permute-done((f32[16,8,512]{2,1,0:T(8,128)S(1)}, f32[16,8,512]{2,1,0:T(8,128)S(1)}, u32[]{:S(2)}, u32[]{:S(2)}) %collective-permute-start.13) | collective-permute-done | bytes 262176 | tf_op jit(solution)/shard_map/while/body/eval_jaxpr/cond/branch_1_fun/ppermute | solution.py:303
  178.9 7.2 %collective-permute-done.15.b_ref = f32[11,16,512]{2,1,0:T(8,128)S(1)} collective-permute-done((f32[11,16,512]{2,1,0:T(8,128)S(1)}, f32[11,16,512]{2,1,0:T(8,128)S(1)}, u32[]{:S(2)}, u32[]{:S(2)}) %collective-permute-start.15) | collective-permute-done | bytes 360480 | tf_op jit(solution)/shard_map/while/body/eval_jaxpr/cond/branch_1_fun/ppermute | solution.py:303
  195.0 12.4 %collective-permute-done.19.r1_ref = f32[16,8,512]{2,1,0:T(8,128)S(1)} collective-permute-done((f32[16,8,512]{2,1,0:T(8,128)S(1)}, f32[16,8,512]{2,1,0:T(8,128)S(1)}, u32[]{:S(2)}, u32[]{:S(2)}) %collective-permute-start.19) | collective-permute-done | bytes 262176 | tf_op jit(solution)/shard_map/while/body/eval_jaxpr/cond/branch_1_fun/ppermute | solution.py:303
  212.5 7.9 %collective-permute-done.21.b_ref = f32[11,16,512]{2,1,0:T(8,128)S(1)} collective-permute-done((f32[11,16,512]{2,1,0:T(8,128)S(1)}, f32[11,16,512]{2,1,0:T(8,128)S(1)}, u32[]{:S(2)}, u32[]{:S(2)}) %collective-permute-start.21) | collective-permute-done | bytes 360480 | tf_op jit(solution)/shard_map/while/body/eval_jaxpr/cond/branch_1_fun/ppermute | solution.py:303
  223.0 72.6 %conditional.2 = (f32[16,8,512]{2,1,0:T(8,128)S(1)}, f32[16,8,512]{2,1,0:T(8,128)S(1)}, f32[16,16,512]{2,1,0:T(8,128)S(1)}) conditional(s32[]{:T(128)} %clamp.10, (s32[1]{0:T(128)}, s32[4]{0:T(128)}, s32[4,3]{1,0:T(4,128)}, f32[4,31]{1,0:T(4,128)}, f32[4,15]{1,0:T(4,128)}, /*index=5*/f32[4,15]{1,0:T(4,128)}, s32[2]{0:T(128)S(1)}, ...), branch_computations={%region_2.2_spmd, %region_3.3_spmd, %region_4.4_spmd} | conditional | flops 6020000256 | bytes 76700784 | solution.py:379
  231.8 8.5 %collective-permute-done.25.r1_ref = f32[16,8,512]{2,1,0:T(8,128)S(1)} collective-permute-done((f32[16,8,512]{2,1,0:T(8,128)S(1)}, f32[16,8,512]{2,1,0:T(8,128)S(1)}, u32[]{:S(2)}, u32[]{:S(2)}) %collective-permute-start.25) | collective-permute-done | bytes 262176 | tf_op jit(solution)/shard_map/while/body/eval_jaxpr/cond/branch_2_fun/ppermute | solution.py:303
  247.7 6.9 %collective-permute-done.27.b_ref = f32[15,16,512]{2,1,0:T(8,128)S(1)} collective-permute-done((f32[15,16,512]{2,1,0:T(8,128)S(1)}, f32[15,16,512]{2,1,0:T(8,128)S(1)}, u32[]{:S(2)}, u32[]{:S(2)}) %collective-permute-start.27) | collective-permute-done | bytes 491552 | tf_op jit(solution)/shard_map/while/body/eval_jaxpr/cond/branch_2_fun/ppermute | solution.py:303
  264.0 16.3 %collective-permute-done.31.r1_ref = f32[16,8,512]{2,1,0:T(8,128)S(1)} collective-permute-done((f32[16,8,512]{2,1,0:T(8,128)S(1)}, f32[16,8,512]{2,1,0:T(8,128)S(1)}, u32[]{:S(2)}, u32[]{:S(2)}) %collective-permute-start.31) | collective-permute-done | bytes 262176 | tf_op jit(solution)/shard_map/while/body/eval_jaxpr/cond/branch_2_fun/ppermute | solution.py:303
  285.5 9.2 %collective-permute-done.33.b_ref = f32[15,16,512]{2,1,0:T(8,128)S(1)} collective-permute-done((f32[15,16,512]{2,1,0:T(8,128)S(1)}, f32[15,16,512]{2,1,0:T(8,128)S(1)}, u32[]{:S(2)}, u32[]{:S(2)}) %collective-permute-start.33) | collective-permute-done | bytes 491552 | tf_op jit(solution)/shard_map/while/body/eval_jaxpr/cond/branch_2_fun/ppermute | solution.py:303
  (156 shorter events, 128.6 us)
Async XLA Ops:
  5.3 18.2 %collective-permute-start.24 = (f32[16,8,512]{2,1,0:T(8,128)S(1)}, f32[16,8,512]{2,1,0:T(8,128)S(1)}, u32[]{:S(2)}, u32[]{:S(2)}) collective-permute-start(f32[16,8,512]{2,1,0:T(8,128)S(1)} %get-tuple-element.335.e0_ref.other0_ref), channel_id=1, source_target_pairs={{0,1},{2,3},{4,5},{6,7},{1,0},{3,2},{5,4},{7,6},{8,9},{10,11},{12,... | collective-permute-start | bytes 786440 | tf_op jit(solution)/shard_map/while/body/eval_jaxpr/cond/branch_2_fun/ppermute | solution.py:303
  6.9 16.6 %collective-permute-start.25 = (f32[16,8,512]{2,1,0:T(8,128)S(1)}, f32[16,8,512]{2,1,0:T(8,128)S(1)}, u32[]{:S(2)}, u32[]{:S(2)}) collective-permute-start(f32[16,8,512]{2,1,0:T(8,128)S(1)} %get-tuple-element.337.e1_ref.other1_ref), channel_id=1, source_target_pairs={{1,2},{3,4},{5,6},{2,1},{4,3},{6,5},{9,10},{11,12},{13,14},{10,9},... | collective-permute-start | bytes 786440 | tf_op jit(solution)/shard_map/while/body/eval_jaxpr/cond/branch_2_fun/ppermute | solution.py:303
  11.8 22.8 %collective-permute-start.28 = (f32[15,16,512]{2,1,0:T(8,128)S(1)}, f32[15,16,512]{2,1,0:T(8,128)S(1)}, u32[]{:S(2)}, u32[]{:S(2)}) collective-permute-start(f32[15,16,512]{2,1,0:T(8,128)S(1)} %get-tuple-element.342), channel_id=1, source_target_pairs={{0,8},{16,24},{32,40},{48,56},{64,72},{80,88},{96,104},{112,120},{... | collective-permute-start | bytes 1474568 | tf_op jit(solution)/shard_map/while/body/eval_jaxpr/cond/branch_2_fun/ppermute | solution.py:303
  11.9 22.7 %collective-permute-start.29 = (f32[15,16,512]{2,1,0:T(8,128)S(1)}, f32[15,16,512]{2,1,0:T(8,128)S(1)}, u32[]{:S(2)}, u32[]{:S(2)}) collective-permute-start(f32[15,16,512]{2,1,0:T(8,128)S(1)} %get-tuple-element.343), channel_id=1, source_target_pairs={{8,16},{24,32},{40,48},{56,64},{72,80},{88,96},{104,112},{120,128}... | collective-permute-start | bytes 1474568 | tf_op jit(solution)/shard_map/while/body/eval_jaxpr/cond/branch_2_fun/ppermute | solution.py:303
  24.7 16.5 %collective-permute-start.27 = (f32[15,16,512]{2,1,0:T(8,128)S(1)}, f32[15,16,512]{2,1,0:T(8,128)S(1)}, u32[]{:S(2)}, u32[]{:S(2)}) collective-permute-start(f32[15,16,512]{2,1,0:T(8,128)S(1)} %get-tuple-element.340), channel_id=1, source_target_pairs={{8,16},{24,32},{40,48},{56,64},{72,80},{88,96},{104,112},{120,128}... | collective-permute-start | bytes 1474568 | tf_op jit(solution)/shard_map/while/body/eval_jaxpr/cond/branch_2_fun/ppermute | solution.py:303
  43.3 20.6 %collective-permute-start.31 = (f32[16,8,512]{2,1,0:T(8,128)S(1)}, f32[16,8,512]{2,1,0:T(8,128)S(1)}, u32[]{:S(2)}, u32[]{:S(2)}) collective-permute-start(f32[16,8,512]{2,1,0:T(8,128)S(1)} %get-tuple-element.346.e1_ref), channel_id=1, source_target_pairs={{1,2},{3,4},{5,6},{2,1},{4,3},{6,5},{9,10},{11,12},{13,14},{10,9},... | collective-permute-start | bytes 786440 | tf_op jit(solution)/shard_map/while/body/eval_jaxpr/cond/branch_2_fun/ppermute | solution.py:303
  49.1 23.0 %collective-permute-start.34 = (f32[15,16,512]{2,1,0:T(8,128)S(1)}, f32[15,16,512]{2,1,0:T(8,128)S(1)}, u32[]{:S(2)}, u32[]{:S(2)}) collective-permute-start(f32[15,16,512]{2,1,0:T(8,128)S(1)} %get-tuple-element.353), channel_id=1, source_target_pairs={{0,8},{16,24},{32,40},{48,56},{64,72},{80,88},{96,104},{112,120},{... | collective-permute-start | bytes 1474568 | tf_op jit(solution)/shard_map/while/body/eval_jaxpr/cond/branch_2_fun/ppermute | solution.py:303
  49.2 22.9 %collective-permute-start.35 = (f32[15,16,512]{2,1,0:T(8,128)S(1)}, f32[15,16,512]{2,1,0:T(8,128)S(1)}, u32[]{:S(2)}, u32[]{:S(2)}) collective-permute-start(f32[15,16,512]{2,1,0:T(8,128)S(1)} %get-tuple-element.354), channel_id=1, source_target_pairs={{8,16},{24,32},{40,48},{56,64},{72,80},{88,96},{104,112},{120,128}... | collective-permute-start | bytes 1474568 | tf_op jit(solution)/shard_map/while/body/eval_jaxpr/cond/branch_2_fun/ppermute | solution.py:303
  82.8 17.0 %collective-permute-start.13 = (f32[16,8,512]{2,1,0:T(8,128)S(1)}, f32[16,8,512]{2,1,0:T(8,128)S(1)}, u32[]{:S(2)}, u32[]{:S(2)}) collective-permute-start(f32[16,8,512]{2,1,0:T(8,128)S(1)} %get-tuple-element.306.e1_ref.other1_ref), channel_id=1, source_target_pairs={{1,2},{3,4},{5,6},{2,1},{4,3},{6,5},{9,10},{11,12},{13,14},{10,9},... | collective-permute-start | bytes 786440 | tf_op jit(solution)/shard_map/while/body/eval_jaxpr/cond/branch_1_fun/ppermute | solution.py:303
  116.4 20.6 %collective-permute-start.19 = (f32[16,8,512]{2,1,0:T(8,128)S(1)}, f32[16,8,512]{2,1,0:T(8,128)S(1)}, u32[]{:S(2)}, u32[]{:S(2)}) collective-permute-start(f32[16,8,512]{2,1,0:T(8,128)S(1)} %get-tuple-element.315.e1_ref), channel_id=1, source_target_pairs={{1,2},{3,4},{5,6},{2,1},{4,3},{6,5},{9,10},{11,12},{13,14},{10,9},... | collective-permute-start | bytes 786440 | tf_op jit(solution)/shard_map/while/body/eval_jaxpr/cond/branch_1_fun/ppermute | solution.py:303
  118.4 21.8 %collective-permute-start.22 = (f32[11,16,512]{2,1,0:T(8,128)S(1)}, f32[11,16,512]{2,1,0:T(8,128)S(1)}, u32[]{:S(2)}, u32[]{:S(2)}) collective-permute-start(f32[11,16,512]{2,1,0:T(8,128)S(1)} %get-tuple-element.322), channel_id=1, source_target_pairs={{0,8},{16,24},{32,40},{48,56},{64,72},{80,88},{96,104},{112,120},{... | collective-permute-start | bytes 1081352 | tf_op jit(solution)/shard_map/while/body/eval_jaxpr/cond/branch_1_fun/ppermute | solution.py:303
  118.5 21.7 %collective-permute-start.23 = (f32[11,16,512]{2,1,0:T(8,128)S(1)}, f32[11,16,512]{2,1,0:T(8,128)S(1)}, u32[]{:S(2)}, u32[]{:S(2)}) collective-permute-start(f32[11,16,512]{2,1,0:T(8,128)S(1)} %get-tuple-element.323), channel_id=1, source_target_pairs={{8,16},{24,32},{40,48},{56,64},{72,80},{88,96},{104,112},{120,128}... | collective-permute-start | bytes 1081352 | tf_op jit(solution)/shard_map/while/body/eval_jaxpr/cond/branch_1_fun/ppermute | solution.py:303
  152.8 20.3 %collective-permute-start.13 = (f32[16,8,512]{2,1,0:T(8,128)S(1)}, f32[16,8,512]{2,1,0:T(8,128)S(1)}, u32[]{:S(2)}, u32[]{:S(2)}) collective-permute-start(f32[16,8,512]{2,1,0:T(8,128)S(1)} %get-tuple-element.306.e1_ref.other1_ref), channel_id=1, source_target_pairs={{1,2},{3,4},{5,6},{2,1},{4,3},{6,5},{9,10},{11,12},{13,14},{10,9},... | collective-permute-start | bytes 786440 | tf_op jit(solution)/shard_map/while/body/eval_jaxpr/cond/branch_1_fun/ppermute | solution.py:303
  156.1 20.1 %collective-permute-start.16 = (f32[11,16,512]{2,1,0:T(8,128)S(1)}, f32[11,16,512]{2,1,0:T(8,128)S(1)}, u32[]{:S(2)}, u32[]{:S(2)}) collective-permute-start(f32[11,16,512]{2,1,0:T(8,128)S(1)} %get-tuple-element.311), channel_id=1, source_target_pairs={{0,8},{16,24},{32,40},{48,56},{64,72},{80,88},{96,104},{112,120},{... | collective-permute-start | bytes 1081352 | tf_op jit(solution)/shard_map/while/body/eval_jaxpr/cond/branch_1_fun/ppermute | solution.py:303
  156.2 20.0 %collective-permute-start.17 = (f32[11,16,512]{2,1,0:T(8,128)S(1)}, f32[11,16,512]{2,1,0:T(8,128)S(1)}, u32[]{:S(2)}, u32[]{:S(2)}) collective-permute-start(f32[11,16,512]{2,1,0:T(8,128)S(1)} %get-tuple-element.312), channel_id=1, source_target_pairs={{8,16},{24,32},{40,48},{56,64},{72,80},{88,96},{104,112},{120,128}... | collective-permute-start | bytes 1081352 | tf_op jit(solution)/shard_map/while/body/eval_jaxpr/cond/branch_1_fun/ppermute | solution.py:303
  188.2 19.1 %collective-permute-start.19 = (f32[16,8,512]{2,1,0:T(8,128)S(1)}, f32[16,8,512]{2,1,0:T(8,128)S(1)}, u32[]{:S(2)}, u32[]{:S(2)}) collective-permute-start(f32[16,8,512]{2,1,0:T(8,128)S(1)} %get-tuple-element.315.e1_ref), channel_id=1, source_target_pairs={{1,2},{3,4},{5,6},{2,1},{4,3},{6,5},{9,10},{11,12},{13,14},{10,9},... | collective-permute-start | bytes 786440 | tf_op jit(solution)/shard_map/while/body/eval_jaxpr/cond/branch_1_fun/ppermute | solution.py:303
  190.2 20.3 %collective-permute-start.22 = (f32[11,16,512]{2,1,0:T(8,128)S(1)}, f32[11,16,512]{2,1,0:T(8,128)S(1)}, u32[]{:S(2)}, u32[]{:S(2)}) collective-permute-start(f32[11,16,512]{2,1,0:T(8,128)S(1)} %get-tuple-element.322), channel_id=1, source_target_pairs={{0,8},{16,24},{32,40},{48,56},{64,72},{80,88},{96,104},{112,120},{... | collective-permute-start | bytes 1081352 | tf_op jit(solution)/shard_map/while/body/eval_jaxpr/cond/branch_1_fun/ppermute | solution.py:303
  190.3 20.2 %collective-permute-start.23 = (f32[11,16,512]{2,1,0:T(8,128)S(1)}, f32[11,16,512]{2,1,0:T(8,128)S(1)}, u32[]{:S(2)}, u32[]{:S(2)}) collective-permute-start(f32[11,16,512]{2,1,0:T(8,128)S(1)} %get-tuple-element.323), channel_id=1, source_target_pairs={{8,16},{24,32},{40,48},{56,64},{72,80},{88,96},{104,112},{120,128}... | collective-permute-start | bytes 1081352 | tf_op jit(solution)/shard_map/while/body/eval_jaxpr/cond/branch_1_fun/ppermute | solution.py:303
  223.1 17.2 %collective-permute-start.25 = (f32[16,8,512]{2,1,0:T(8,128)S(1)}, f32[16,8,512]{2,1,0:T(8,128)S(1)}, u32[]{:S(2)}, u32[]{:S(2)}) collective-permute-start(f32[16,8,512]{2,1,0:T(8,128)S(1)} %get-tuple-element.337.e1_ref.other1_ref), channel_id=1, source_target_pairs={{1,2},{3,4},{5,6},{2,1},{4,3},{6,5},{9,10},{11,12},{13,14},{10,9},... | collective-permute-start | bytes 786440 | tf_op jit(solution)/shard_map/while/body/eval_jaxpr/cond/branch_2_fun/ppermute | solution.py:303
  226.5 17.0 %collective-permute-start.28 = (f32[15,16,512]{2,1,0:T(8,128)S(1)}, f32[15,16,512]{2,1,0:T(8,128)S(1)}, u32[]{:S(2)}, u32[]{:S(2)}) collective-permute-start(f32[15,16,512]{2,1,0:T(8,128)S(1)} %get-tuple-element.342), channel_id=1, source_target_pairs={{0,8},{16,24},{32,40},{48,56},{64,72},{80,88},{96,104},{112,120},{... | collective-permute-start | bytes 1474568 | tf_op jit(solution)/shard_map/while/body/eval_jaxpr/cond/branch_2_fun/ppermute | solution.py:303
  226.6 18.4 %collective-permute-start.29 = (f32[15,16,512]{2,1,0:T(8,128)S(1)}, f32[15,16,512]{2,1,0:T(8,128)S(1)}, u32[]{:S(2)}, u32[]{:S(2)}) collective-permute-start(f32[15,16,512]{2,1,0:T(8,128)S(1)} %get-tuple-element.343), channel_id=1, source_target_pairs={{8,16},{24,32},{40,48},{56,64},{72,80},{88,96},{104,112},{120,128}... | collective-permute-start | bytes 1474568 | tf_op jit(solution)/shard_map/while/body/eval_jaxpr/cond/branch_2_fun/ppermute | solution.py:303
  259.6 20.7 %collective-permute-start.31 = (f32[16,8,512]{2,1,0:T(8,128)S(1)}, f32[16,8,512]{2,1,0:T(8,128)S(1)}, u32[]{:S(2)}, u32[]{:S(2)}) collective-permute-start(f32[16,8,512]{2,1,0:T(8,128)S(1)} %get-tuple-element.346.e1_ref), channel_id=1, source_target_pairs={{1,2},{3,4},{5,6},{2,1},{4,3},{6,5},{9,10},{11,12},{13,14},{10,9},... | collective-permute-start | bytes 786440 | tf_op jit(solution)/shard_map/while/body/eval_jaxpr/cond/branch_2_fun/ppermute | solution.py:303
  261.5 22.0 %collective-permute-start.34 = (f32[15,16,512]{2,1,0:T(8,128)S(1)}, f32[15,16,512]{2,1,0:T(8,128)S(1)}, u32[]{:S(2)}, u32[]{:S(2)}) collective-permute-start(f32[15,16,512]{2,1,0:T(8,128)S(1)} %get-tuple-element.353), channel_id=1, source_target_pairs={{0,8},{16,24},{32,40},{48,56},{64,72},{80,88},{96,104},{112,120},{... | collective-permute-start | bytes 1474568 | tf_op jit(solution)/shard_map/while/body/eval_jaxpr/cond/branch_2_fun/ppermute | solution.py:303
  261.6 21.9 %collective-permute-start.35 = (f32[15,16,512]{2,1,0:T(8,128)S(1)}, f32[15,16,512]{2,1,0:T(8,128)S(1)}, u32[]{:S(2)}, u32[]{:S(2)}) collective-permute-start(f32[15,16,512]{2,1,0:T(8,128)S(1)} %get-tuple-element.354), channel_id=1, source_target_pairs={{8,16},{24,32},{40,48},{56,64},{72,80},{88,96},{104,112},{120,128}... | collective-permute-start | bytes 1474568 | tf_op jit(solution)/shard_map/while/body/eval_jaxpr/cond/branch_2_fun/ppermute | solution.py:303
  (33 other events, 366.1 us)

commit v2 on v1

--- a/solution.py
+++ b/solution.py
@@ -12,7 +12,7 @@
 REACH_L = 7
 TAPS_Z = 2 * REACH_Z + 1
 TAPS_L = 2 * REACH_L + 1
-REACHES = (7, 11, 15)
+REACHES = (6, 9, 12, 15)
 F32 = jnp.float32
 BF16 = jnp.bfloat16
 
@@ -100,7 +100,21 @@
     return banded(jnp.where((r >> 4) == zc, yi - yo + REACH_L, -1), table)
 
 
-def prepare_kernel(planes, pos_ref, order_ref, extents_ref, psf_z_ref, psf_y_ref, psf_x_ref, par_ref, ye_ref, ym_ref, z_ref, x_ref):
+def prepare_first_kernel(pos_ref, order_ref, extents_ref, psf_y_ref, par_ref, ye_ref):
+    hi, lo = edge_bands(tap_table(psf_y_ref, extents_ref, order_ref, pos_ref[0], 0, 1, TAPS_L), par_ref[1])
+    ye_ref[:64, :] = hi
+    ye_ref[64:, :] = lo
+
+
+def prepare_rest_kernel(planes, pos_ref, order_ref, extents_ref, psf_z_ref, psf_y_ref, psf_x_ref, par_ref, after_ref,
+                        ye_ref, ym_ref, z_ref, x_ref):
+    table = tap_table(psf_y_ref, extents_ref, order_ref, pos_ref[0], 1, 1, TAPS_L)
+    hi, lo = edge_bands(table, par_ref[1])
+    ye_ref[:64, :] = hi
+    ye_ref[64:, :] = lo
+    hi, lo = middle_bands(table, par_ref[1])
+    ym_ref[:128, :] = hi
+    ym_ref[128:, :] = lo
     par = par_ref[0]
     pos = pos_ref[0]
     tall = 8 * planes
@@ -108,14 +122,6 @@
     blocks = x_ref.shape[-1] // 128
 
     def one(flip, carry):
-        table = tap_table(psf_y_ref, extents_ref, order_ref, pos, flip, 1, TAPS_L)
-        hi, lo = edge_bands(table, par_ref[1])
-        ye_ref[flip, :64, :] = hi
-        ye_ref[flip, 64:, :] = lo
-        hi, lo = middle_bands(table, par_ref[1])
-        ym_ref[flip, :128, :] = hi
-        ym_ref[flip, 128:, :] = lo
-
         table = tap_table(psf_z_ref, extents_ref, order_ref, pos, flip, 0, TAPS_Z)
 
         def z_rows(chunk, inner):
@@ -174,7 +180,7 @@
     planes, half, width = out_ref.shape
     split = 16 * planes
     for g in range(0, half, 8):
-        x = tall_rows(planes, own_ref[:, g:g + 8, :], a_ref[:, g:g + 8, :])
+        x = tall_rows(planes, own_ref[:, g:g + 8, :], a_ref[:, 16 + g:24 + g, :])
         out_ref[:, g:g + 8, :] = stacked(wz[:, :split], x).reshape(planes, 8, width)
 
 
@@ -189,18 +195,34 @@
 
 def zx_stage(wz, wx, own_ref, a_ref, b_ref, z_buf):
     planes, half, width = z_buf.shape
-    for g in range(0, half, 8):
-        x = tall_rows(planes, own_ref[:, g:g + 8, :], a_ref[:, g:g + 8, :], b_ref[:, g:g + 8, :])
-        z_buf[:, g:g + 8, :] = stacked(wz, x).reshape(planes, 8, width)
+
+    def one(group, carry):
+        rows = pl.ds(pl.multiple_of(8 * group, 8), 8)
+        x = tall_rows(planes, own_ref[:, rows, :], a_ref[:, rows, :], b_ref[:, rows, :])
+        z_buf[:, rows, :] = stacked(wz, x).reshape(planes, 8, width)
+        return carry
+
+    lax.fori_loop(0, half // 8, one, 0)
     return x_stage(wx, z_buf[...].reshape(planes * half, width)).reshape(z_buf.shape)
 
 
-def send_parts(par, whole_ref, a_ref, b_ref):
+def send_outer(par, whole_ref, b_ref):
     last = whole_ref.shape[0] - 1
 
     def one(j, carry):
         b_ref[j] = whole_ref[jnp.where(par == 1, last - j, j)]
-        a_ref[j] = whole_ref[jnp.where(par == 1, j, last - j)]
+        return carry
+
+    lax.fori_loop(0, b_ref.shape[0], one, 0)
+
+
+def send_inner(par, middle_ref, edge_ref, a_ref):
+    last = middle_ref.shape[0] - 1
+
+    def one(j, carry):
+        plane = jnp.where(par == 1, j, last - j)
+        a_ref[j, :16, :] = middle_ref[plane]
+        a_ref[j, 16:, :] = edge_ref[plane]
         return carry
 
     lax.fori_loop(0, a_ref.shape[0], one, 0)
@@ -239,21 +261,22 @@
     out_ref[:, 8:24, :] = m_ref[...]
 
 
-def open_kernel(pos_ref, order_ref, extents_ref, psf_ref, par_ref, e0_ref, m_ref, e1_ref, ny_ref, na_ref, nb_ref, w_buf):
+def open_kernel(pos_ref, order_ref, extents_ref, psf_ref, par_ref, e0_ref, m_ref, e1_ref, ny_ref, nb_ref, w_buf):
     hi, lo = middle_bands(tap_table(psf_ref, extents_ref, order_ref, pos_ref[0], 0, 1, TAPS_L), par_ref[1])
     w_buf[:128, :] = hi
     w_buf[128:, :] = lo
     y_middle(w_buf[...], e0_ref, m_ref, e1_ref, ny_ref)
-    send_parts(par_ref[0], ny_ref, na_ref, nb_ref)
-
-
-def edge_y_kernel(flip, par_ref, ye_ref, e0_ref, m_ref, e1_ref, r0_ref, r1_ref, ny_ref, na_ref, nb_ref):
+    send_outer(par_ref[0], ny_ref, nb_ref)
+
+
+def edge_y_kernel(par_ref, ye_ref, e0_ref, m_ref, e1_ref, r0_ref, r1_ref, middle_ref, ny_ref, na_ref, nb_ref):
     for q in range(0, m_ref.shape[0], 4):
         pieces = []
         for z in range(q, q + 4):
             pieces += [r[z] for r in (r0_ref, e0_ref, m_ref, e1_ref, r1_ref)]
-        ny_ref[q:q + 4] = stacked(ye_ref[flip], jnp.concatenate(pieces, axis=0)).reshape(4, 16, m_ref.shape[-1])
-    send_parts(par_ref[0], ny_ref, na_ref, nb_ref)
+        ny_ref[q:q + 4] = stacked(ye_ref[...], jnp.concatenate(pieces, axis=0)).reshape(4, 16, m_ref.shape[-1])
+    send_outer(par_ref[0], ny_ref, nb_ref)
+    send_inner(par_ref[0], middle_ref, ny_ref, na_ref)
 
 
 def inner_kernel(flip, wz_ref, own_ref, a_ref, out_ref):
@@ -273,7 +296,7 @@
 
 
 def forward_edge_kernel(par_ref, pos_ref, order_ref, wz_ref, wx_ref, ym_ref, inner_ref, b_ref, m_ref, measured_ref,
-                        e0_ref, e1_ref, ny_ref, na_ref, nb_ref, z_buf, m_buf, sems):
+                        e0_ref, e1_ref, ny_ref, nb_ref, z_buf, m_buf, sems):
     first, last = edge_rows(par_ref[1])
     view = order_ref[pos_ref[0]]
     copies = [
@@ -287,8 +310,8 @@
         copy.wait()
     e0_ref[...] = m_buf[:, :8, :] / result[:, :8]
     e1_ref[...] = m_buf[:, 8:, :] / result[:, 8:]
-    y_middle(ym_ref[1], e0_ref, m_ref, e1_ref, ny_ref)
-    send_parts(par_ref[0], ny_ref, na_ref, nb_ref)
+    y_middle(ym_ref[...], e0_ref, m_ref, e1_ref, ny_ref)
+    send_outer(par_ref[0], ny_ref, nb_ref)
 
 
 def adjoint_edge_kernel(wz_ref, wx_ref, inner_ref, b_ref, other0_ref, other1_ref, e0_ref, e1_ref, z_buf):
@@ -320,34 +343,37 @@
     planes, _, width = half.shape
     order, extents, psf_z, psf_y, psf_x = tables
     part = jax.ShapeDtypeStruct((reach, 16, width), F32)
+    both = jax.ShapeDtypeStruct((reach, 32, width), F32)
     dma = pltpu.SemaphoreType.DMA
     z_buf = pltpu.VMEM(half.shape, F32)
     m_buf = pltpu.VMEM(half.shape, F32)
     sm, vm = SMEM_SPEC, VMEM_SPEC
 
-    ny, na, nb = call(open_kernel, [sm] * 5 + [vm] * 3, [half, part, part], 200_000_000,
+    ny, nb = call(open_kernel, [sm] * 5 + [vm] * 3, [half, part], 200_000_000,
                       [pltpu.VMEM((256, 256), BF16)])(pos, order, extents, psf_y, parity, e0, m, e1)
-    weights = [jax.ShapeDtypeStruct((2,) + s, BF16)
-               for s in ((128, 192), (256, 256), (16 * planes, 24 * planes), (2, width, width))]
-    mye, mym, mz, mx = call(functools.partial(prepare_kernel, planes), [sm] * 7, weights, 20_000_000, mib=8)(
-        pos, order, extents, psf_z, psf_y, psf_x, parity)
+    wye, wym, wz, wx = [jax.ShapeDtypeStruct(s, BF16)
+                        for s in ((128, 192), (256, 256), (2, 16 * planes, 24 * planes), (2, 2, width, width))]
+    mye, = call(prepare_first_kernel, [sm] * 5, [wye], 1_000_000, mib=8)(pos, order, extents, psf_y, parity)
     current = (e0, e1, m)
     for flip in (0, 1):
         r1 = pair_exchange(e1, "gy", 1)
         bm = pair_exchange(nb, "gz", 1)
         r0 = pair_exchange(e0, "gy", 0)
-        am = pair_exchange(na, "gz", 0)
-        ey, ea, eb = call(functools.partial(edge_y_kernel, flip), [sm] + [vm] * 6, [half, part, part],
-                          400_000_000)(parity, mye, e0, m, e1, r0, r1)
+        ey, ea, eb = call(edge_y_kernel, [sm] + [vm] * 7, [half, both, part],
+                          400_000_000)(parity, mye, e0, m, e1, r0, r1, ny)
+        if flip == 0:
+            mye, mym, mz, mx = call(functools.partial(prepare_rest_kernel, planes), [sm] * 7 + [ANY_SPEC],
+                                    [wye, wym, wz, wx], 20_000_000, mib=8)(
+                pos, order, extents, psf_z, psf_y, psf_x, parity, ey)
         be = pair_exchange(eb, "gz", 1)
         ae = pair_exchange(ea, "gz", 0)
         m, = call(functools.partial(middle_kernel, flip), [sm] * 2 + [vm] * 5 + [vm if flip else ANY_SPEC],
                   [half], 1_000_000_000, [z_buf, m_buf, dma((1,))])(
-            pos, order, mz, mx, ny, am, bm, current[2] if flip else measured)
+            pos, order, mz, mx, ny, ae, bm, current[2] if flip else measured)
         inner, = call(functools.partial(inner_kernel, flip), [vm] * 3, [half], 400_000_000)(mz, ey, ae)
         if flip == 0:
-            e0, e1, ny, na, nb = call(forward_edge_kernel, [sm] * 3 + [vm] * 6 + [ANY_SPEC],
-                                      [group, group, half, part, part], 1_200_000_000, [z_buf, m_buf, dma((2,))])(
+            e0, e1, ny, nb = call(forward_edge_kernel, [sm] * 3 + [vm] * 6 + [ANY_SPEC],
+                                      [group, group, half, part], 1_200_000_000, [z_buf, m_buf, dma((2,))])(
                 parity, pos, order, mz, mx, mym, inner, be, m, measured)
         else:
             e0, e1 = call(adjoint_edge_kernel, [vm] * 6, [group, group], 1_000_000_000, [z_buf])(
@@ -366,11 +392,12 @@
     tables = (order, extents, psf_z, psf_y, psf_x)
     radii = (extents[:, 0] - 1) // 2
     sizes = sum((radii > r).astype(jnp.int32) for r in REACHES[:-1]) if len(REACHES) > 1 else jnp.zeros_like(radii)
-
+    places = 2 * jnp.arange(views, dtype=jnp.int32)[:, None]
+    chosen = order[:, None] == jnp.arange(views, dtype=jnp.int32)[None, :]
+    packed = jnp.sum(jnp.where(chosen, sizes[None, :] << places, 0))
     state = call(split_kernel, [SMEM_SPEC, ANY_SPEC], [group, group, half], 1, [pltpu.SemaphoreType.DMA((3,))])(
         parity, estimate)
     passes = [functools.partial(view_pass, r, (group, half), parity, tables, measured) for r in reaches]
-    packed = jnp.sum(sizes[order] << (2 * jnp.arange(views, dtype=jnp.int32)))
 
     def step(index, state):
         pos = jnp.reshape(index, (1,)).astype(jnp.int32)

time: 299 us -> 327 us (1.094)
  the two profiles are of different devices: /device:TPU:40 before, /device:TPU:121 now
where the time goes in v2:
time: 327 us; the launch traced here: 326 us
  waiting for transfers between devices  130 us (40%)
  starting transfers between devices  121 us (37%)
  Pallas kernels  62.7 us (19%)
  loops' own time  8.36 us (3%)
    ppermute x40, waiting for transfers between devices, pair_exchange(): return lax.ppermute(value, axis, pairs + [(j, i) for i, j in pairs])  130 us
    ppermute x40, starting transfers between devices, pair_exchange(): return lax.ppermute(value, axis, pairs + [(j, i) for i, j in pairs])  121 us
    pallas_call x8, Pallas kernels, view_pass(): call(functools.partial(middle_kernel, flip), [sm] * 2 + [vm] * 5 + [vm if...  15.4 us
    pallas_call x4, Pallas kernels, view_pass(): call(functools.partial(prepare_rest_kernel, planes), [sm] * 7 + [ANY_SPEC...  12.4 us
    pallas_call x8, Pallas kernels, view_pass(): call(edge_y_kernel, [sm] + [vm] * 7, [half, both, part], 400000000)  9.27 us
    pallas_call x4, Pallas kernels, view_pass(): call(forward_edge_kernel, [sm] * 3 + [vm] * 6 + [ANY_SPEC], [group, group...  7.96 us
    another operation x1, loops' own time, on_device(): state = lax.fori_loop(0, views, step, (packed, *state))[1:]  7.2 us
  transfers between devices with their start and end apart: 40, of which 29 were waited for; matrix products, arithmetic and copies ran while one was open for 0% of the time, Pallas kernels for 12%

profile of v2, /device:TPU:121, one launch (start us, length us, event | category | flops | bytes accessed | tf_op | source)
XLA Modules:
  0.0 325.8 jit_solution(8659182453068159637)
XLA Ops:
  4.2 320.0 %while.19 = (s32[]{:T(128)}, s32[]{:T(128)}, f32[16,8,512]{2,1,0:T(8,128)S(1)}, f32[16,8,512]{2,1,0:T(8,128)S(1)}, f32[16,16,512]{2,1,0:T(8,128)S(1)}, /*index=5...) while((s32[]{:T(128)}, s32[]{:T(128)}, ...), condition=%wide.region_6.7_spmd, body=%wide.region_1.6_spmd.sunk | while | flops 6020999680 | bytes 82802344 | solution.py:408
  4.8 82.2 %conditional.2 = (f32[16,8,512]{2,1,0:T(8,128)S(1)}, f32[16,8,512]{2,1,0:T(8,128)S(1)}, f32[16,16,512]{2,1,0:T(8,128)S(1)}) conditional(s32[]{:T(128)} %clamp.8, (s32[1]{0:T(128)}, s32[4]{0:T(128)}, s32[4,3]{1,0:T(4,128)}, f32[4,15]{1,0:T(4,128)}, s32[2]{0:T(128)S(1)}, /*index=5*/f32[16,8,512]{2,1,0:T(8,128)S(1)}, ...), branch_computations={%region_2.2_spmd, %region_3.3_spmd, %region_4.4_spmd, %region_5.5_... | conditional | flops 6020999680 | bytes 80704912 | solution.py:406
  12.2 4.9 %collective-permute-done.31.r1_ref = f32[16,8,512]{2,1,0:T(8,128)S(1)} collective-permute-done((f32[16,8,512]{2,1,0:T(8,128)S(1)}, f32[16,8,512]{2,1,0:T(8,128)S(1)}, u32[]{:S(2)}, u32[]{:S(2)}) %collective-permute-start.31) | collective-permute-done | bytes 262176 | tf_op jit(solution)/shard_map/while/body/eval_jaxpr/cond/branch_3_fun/ppermute | solution.py:326
  20.2 5.1 %collective-permute-start.34 = (f32[15,16,512]{2,1,0:T(8,128)S(1)}, f32[15,16,512]{2,1,0:T(8,128)S(1)}, u32[]{:S(2)}, u32[]{:S(2)}) collective-permute-start(f32[15,16,512]{2,1,0:T(8,128)S(1)} %get-tuple-element.389), channel_id=1, source_target_pairs={{8,16},{24,32},{40,48},{56,64},{72,80},{88,96},{104,112},{120,128}... | collective-permute-start | bytes 1474568 | tf_op jit(solution)/shard_map/while/body/eval_jaxpr/cond/branch_3_fun/ppermute | solution.py:326
  31.4 6.4 %collective-permute-done.34.b_ref = f32[15,16,512]{2,1,0:T(8,128)S(1)} collective-permute-done((f32[15,16,512]{2,1,0:T(8,128)S(1)}, f32[15,16,512]{2,1,0:T(8,128)S(1)}, u32[]{:S(2)}, u32[]{:S(2)}) %collective-permute-start.34) | collective-permute-done | bytes 491552 | tf_op jit(solution)/shard_map/while/body/eval_jaxpr/cond/branch_3_fun/ppermute | solution.py:326
  39.9 4.5 %collective-permute-done.33.b_ref = f32[15,16,512]{2,1,0:T(8,128)S(1)} collective-permute-done((f32[15,16,512]{2,1,0:T(8,128)S(1)}, f32[15,16,512]{2,1,0:T(8,128)S(1)}, u32[]{:S(2)}, u32[]{:S(2)}) %collective-permute-start.33) | collective-permute-done | bytes 491552 | tf_op jit(solution)/shard_map/while/body/eval_jaxpr/cond/branch_3_fun/ppermute | solution.py:326
  46.5 6.2 %collective-permute-start.36 = (f32[16,8,512]{2,1,0:T(8,128)S(1)}, f32[16,8,512]{2,1,0:T(8,128)S(1)}, u32[]{:S(2)}, u32[]{:S(2)}) collective-permute-start(f32[16,8,512]{2,1,0:T(8,128)S(1)} %get-tuple-element.392.e1_ref), channel_id=1, source_target_pairs={{1,2},{3,4},{5,6},{2,1},{4,3},{6,5},{9,10},{11,12},{13,14},{10,9},... | collective-permute-start | bytes 786440 | tf_op jit(solution)/shard_map/while/body/eval_jaxpr/cond/branch_3_fun/ppermute | solution.py:326
  61.2 6.0 %collective-permute-start.39 = (f32[15,16,512]{2,1,0:T(8,128)S(1)}, f32[15,16,512]{2,1,0:T(8,128)S(1)}, u32[]{:S(2)}, u32[]{:S(2)}) collective-permute-start(f32[15,16,512]{2,1,0:T(8,128)S(1)} %get-tuple-element.399), channel_id=1, source_target_pairs={{8,16},{24,32},{40,48},{56,64},{72,80},{88,96},{104,112},{120,128}... | collective-permute-start | bytes 1474568 | tf_op jit(solution)/shard_map/while/body/eval_jaxpr/cond/branch_3_fun/ppermute | solution.py:326
  69.5 11.3 %collective-permute-done.39.b_ref = f32[15,16,512]{2,1,0:T(8,128)S(1)} collective-permute-done((f32[15,16,512]{2,1,0:T(8,128)S(1)}, f32[15,16,512]{2,1,0:T(8,128)S(1)}, u32[]{:S(2)}, u32[]{:S(2)}) %collective-permute-start.39) | collective-permute-done | bytes 491552 | tf_op jit(solution)/shard_map/while/body/eval_jaxpr/cond/branch_3_fun/ppermute | solution.py:326
  88.9 74.2 %conditional.2 = (f32[16,8,512]{2,1,0:T(8,128)S(1)}, f32[16,8,512]{2,1,0:T(8,128)S(1)}, f32[16,16,512]{2,1,0:T(8,128)S(1)}) conditional(s32[]{:T(128)} %clamp.8, (s32[1]{0:T(128)}, s32[4]{0:T(128)}, s32[4,3]{1,0:T(4,128)}, f32[4,15]{1,0:T(4,128)}, s32[2]{0:T(128)S(1)}, /*index=5*/f32[16,8,512]{2,1,0:T(8,128)S(1)}, ...), branch_computations={%region_2.2_spmd, %region_3.3_spmd, %region_4.4_spmd, %region_5.5_... | conditional | flops 6020999680 | bytes 80704912 | solution.py:406
  89.0 5.4 %collective-permute-start.11 = (f32[16,8,512]{2,1,0:T(8,128)S(1)}, f32[16,8,512]{2,1,0:T(8,128)S(1)}, u32[]{:S(2)}, u32[]{:S(2)}) collective-permute-start(f32[16,8,512]{2,1,0:T(8,128)S(1)} %get-tuple-element.322.e1_ref.other1_ref), channel_id=1, source_target_pairs={{1,2},{3,4},{5,6},{2,1},{4,3},{6,5},{9,10},{11,12},{13,14},{10,9},... | collective-permute-start | bytes 786440 | tf_op jit(solution)/shard_map/while/body/eval_jaxpr/cond/branch_1_fun/ppermute | solution.py:326
  101.6 14.1 %collective-permute-start.14 = (f32[9,16,512]{2,1,0:T(8,128)S(1)}, f32[9,16,512]{2,1,0:T(8,128)S(1)}, u32[]{:S(2)}, u32[]{:S(2)}) collective-permute-start(f32[9,16,512]{2,1,0:T(8,128)S(1)} %get-tuple-element.331), channel_id=1, source_target_pairs={{8,16},{24,32},{40,48},{56,64},{72,80},{88,96},{104,112},{120,128}... | collective-permute-start | bytes 884744 | tf_op jit(solution)/shard_map/while/body/eval_jaxpr/cond/branch_1_fun/ppermute | solution.py:326
  133.2 7.2 %collective-permute-done.16.r1_ref = f32[16,8,512]{2,1,0:T(8,128)S(1)} collective-permute-done((f32[16,8,512]{2,1,0:T(8,128)S(1)}, f32[16,8,512]{2,1,0:T(8,128)S(1)}, u32[]{:S(2)}, u32[]{:S(2)}) %collective-permute-start.16) | collective-permute-done | bytes 262176 | tf_op jit(solution)/shard_map/while/body/eval_jaxpr/cond/branch_1_fun/ppermute | solution.py:326
  141.6 10.5 %collective-permute-start.19 = (f32[9,16,512]{2,1,0:T(8,128)S(1)}, f32[9,16,512]{2,1,0:T(8,128)S(1)}, u32[]{:S(2)}, u32[]{:S(2)}) collective-permute-start(f32[9,16,512]{2,1,0:T(8,128)S(1)} %get-tuple-element.341), channel_id=1, source_target_pairs={{8,16},{24,32},{40,48},{56,64},{72,80},{88,96},{104,112},{120,128}... | collective-permute-start | bytes 884744 | tf_op jit(solution)/shard_map/while/body/eval_jaxpr/cond/branch_1_fun/ppermute | solution.py:326
  165.0 70.5 %conditional.2 = (f32[16,8,512]{2,1,0:T(8,128)S(1)}, f32[16,8,512]{2,1,0:T(8,128)S(1)}, f32[16,16,512]{2,1,0:T(8,128)S(1)}) conditional(s32[]{:T(128)} %clamp.8, (s32[1]{0:T(128)}, s32[4]{0:T(128)}, s32[4,3]{1,0:T(4,128)}, f32[4,15]{1,0:T(4,128)}, s32[2]{0:T(128)S(1)}, /*index=5*/f32[16,8,512]{2,1,0:T(8,128)S(1)}, ...), branch_computations={%region_2.2_spmd, %region_3.3_spmd, %region_4.4_spmd, %region_5.5_... | conditional | flops 6020999680 | bytes 80704912 | solution.py:406
  170.4 10.3 %collective-permute-done.11.r1_ref = f32[16,8,512]{2,1,0:T(8,128)S(1)} collective-permute-done((f32[16,8,512]{2,1,0:T(8,128)S(1)}, f32[16,8,512]{2,1,0:T(8,128)S(1)}, u32[]{:S(2)}, u32[]{:S(2)}) %collective-permute-start.11) | collective-permute-done | bytes 262176 | tf_op jit(solution)/shard_map/while/body/eval_jaxpr/cond/branch_1_fun/ppermute | solution.py:326
  181.9 6.9 %collective-permute-start.14 = (f32[9,16,512]{2,1,0:T(8,128)S(1)}, f32[9,16,512]{2,1,0:T(8,128)S(1)}, u32[]{:S(2)}, u32[]{:S(2)}) collective-permute-start(f32[9,16,512]{2,1,0:T(8,128)S(1)} %get-tuple-element.331), channel_id=1, source_target_pairs={{8,16},{24,32},{40,48},{56,64},{72,80},{88,96},{104,112},{120,128}... | collective-permute-start | bytes 884744 | tf_op jit(solution)/shard_map/while/body/eval_jaxpr/cond/branch_1_fun/ppermute | solution.py:326
  206.6 10.1 %collective-permute-done.16.r1_ref = f32[16,8,512]{2,1,0:T(8,128)S(1)} collective-permute-done((f32[16,8,512]{2,1,0:T(8,128)S(1)}, f32[16,8,512]{2,1,0:T(8,128)S(1)}, u32[]{:S(2)}, u32[]{:S(2)}) %collective-permute-start.16) | collective-permute-done | bytes 262176 | tf_op jit(solution)/shard_map/while/body/eval_jaxpr/cond/branch_1_fun/ppermute | solution.py:326
  217.9 6.5 %collective-permute-start.19 = (f32[9,16,512]{2,1,0:T(8,128)S(1)}, f32[9,16,512]{2,1,0:T(8,128)S(1)}, u32[]{:S(2)}, u32[]{:S(2)}) collective-permute-start(f32[9,16,512]{2,1,0:T(8,128)S(1)} %get-tuple-element.341), channel_id=1, source_target_pairs={{8,16},{24,32},{40,48},{56,64},{72,80},{88,96},{104,112},{120,128}... | collective-permute-start | bytes 884744 | tf_op jit(solution)/shard_map/while/body/eval_jaxpr/cond/branch_1_fun/ppermute | solution.py:326
  237.3 85.6 %conditional.2 = (f32[16,8,512]{2,1,0:T(8,128)S(1)}, f32[16,8,512]{2,1,0:T(8,128)S(1)}, f32[16,16,512]{2,1,0:T(8,128)S(1)}) conditional(s32[]{:T(128)} %clamp.8, (s32[1]{0:T(128)}, s32[4]{0:T(128)}, s32[4,3]{1,0:T(4,128)}, f32[4,15]{1,0:T(4,128)}, s32[2]{0:T(128)S(1)}, /*index=5*/f32[16,8,512]{2,1,0:T(8,128)S(1)}, ...), branch_computations={%region_2.2_spmd, %region_3.3_spmd, %region_4.4_spmd, %region_5.5_... | conditional | flops 6020999680 | bytes 80704912 | solution.py:406
  243.0 14.3 %collective-permute-done.31.r1_ref = f32[16,8,512]{2,1,0:T(8,128)S(1)} collective-permute-done((f32[16,8,512]{2,1,0:T(8,128)S(1)}, f32[16,8,512]{2,1,0:T(8,128)S(1)}, u32[]{:S(2)}, u32[]{:S(2)}) %collective-permute-start.31) | collective-permute-done | bytes 262176 | tf_op jit(solution)/shard_map/while/body/eval_jaxpr/cond/branch_3_fun/ppermute | solution.py:326
  258.6 6.7 %collective-permute-start.34 = (f32[15,16,512]{2,1,0:T(8,128)S(1)}, f32[15,16,512]{2,1,0:T(8,128)S(1)}, u32[]{:S(2)}, u32[]{:S(2)}) collective-permute-start(f32[15,16,512]{2,1,0:T(8,128)S(1)} %get-tuple-element.389), channel_id=1, source_target_pairs={{8,16},{24,32},{40,48},{56,64},{72,80},{88,96},{104,112},{120,128}... | collective-permute-start | bytes 1474568 | tf_op jit(solution)/shard_map/while/body/eval_jaxpr/cond/branch_3_fun/ppermute | solution.py:326
  281.6 4.6 %collective-permute-done.35.r0_ref = f32[16,8,512]{2,1,0:T(8,128)S(1)} collective-permute-done((f32[16,8,512]{2,1,0:T(8,128)S(1)}, f32[16,8,512]{2,1,0:T(8,128)S(1)}, u32[]{:S(2)}, u32[]{:S(2)}) %collective-permute-start.35) | collective-permute-done | bytes 262176 | tf_op jit(solution)/shard_map/while/body/eval_jaxpr/cond/branch_3_fun/ppermute | solution.py:326
  291.3 18.5 %collective-permute-start.39 = (f32[15,16,512]{2,1,0:T(8,128)S(1)}, f32[15,16,512]{2,1,0:T(8,128)S(1)}, u32[]{:S(2)}, u32[]{:S(2)}) collective-permute-start(f32[15,16,512]{2,1,0:T(8,128)S(1)} %get-tuple-element.399), channel_id=1, source_target_pairs={{8,16},{24,32},{40,48},{56,64},{72,80},{88,96},{104,112},{120,128}... | collective-permute-start | bytes 1474568 | tf_op jit(solution)/shard_map/while/body/eval_jaxpr/cond/branch_3_fun/ppermute | solution.py:326
  (173 shorter events, 157.9 us)
Async XLA Ops:
  18.3 12.7 %collective-permute-start.32 = (f32[15,32,512]{2,1,0:T(8,128)S(1)}, f32[15,32,512]{2,1,0:T(8,128)S(1)}, u32[]{:S(2)}, u32[]{:S(2)}) collective-permute-start(f32[15,32,512]{2,1,0:T(8,128)S(1)} %get-tuple-element.387), channel_id=1, source_target_pairs={{0,8},{16,24},{32,40},{48,56},{64,72},{80,88},{96,104},{112,120},{... | collective-permute-start | bytes 2949128 | tf_op jit(solution)/shard_map/while/body/eval_jaxpr/cond/branch_3_fun/ppermute | solution.py:326
  20.2 17.7 %collective-permute-start.34 = (f32[15,16,512]{2,1,0:T(8,128)S(1)}, f32[15,16,512]{2,1,0:T(8,128)S(1)}, u32[]{:S(2)}, u32[]{:S(2)}) collective-permute-start(f32[15,16,512]{2,1,0:T(8,128)S(1)} %get-tuple-element.389), channel_id=1, source_target_pairs={{8,16},{24,32},{40,48},{56,64},{72,80},{88,96},{104,112},{120,128}... | collective-permute-start | bytes 1474568 | tf_op jit(solution)/shard_map/while/body/eval_jaxpr/cond/branch_3_fun/ppermute | solution.py:326
  25.3 19.1 %collective-permute-start.33 = (f32[15,16,512]{2,1,0:T(8,128)S(1)}, f32[15,16,512]{2,1,0:T(8,128)S(1)}, u32[]{:S(2)}, u32[]{:S(2)}) collective-permute-start(f32[15,16,512]{2,1,0:T(8,128)S(1)} %get-tuple-element.388), channel_id=1, source_target_pairs={{8,16},{24,32},{40,48},{56,64},{72,80},{88,96},{104,112},{120,128}... | collective-permute-start | bytes 1474568 | tf_op jit(solution)/shard_map/while/body/eval_jaxpr/cond/branch_3_fun/ppermute | solution.py:326
  46.5 12.1 %collective-permute-start.36 = (f32[16,8,512]{2,1,0:T(8,128)S(1)}, f32[16,8,512]{2,1,0:T(8,128)S(1)}, u32[]{:S(2)}, u32[]{:S(2)}) collective-permute-start(f32[16,8,512]{2,1,0:T(8,128)S(1)} %get-tuple-element.392.e1_ref), channel_id=1, source_target_pairs={{1,2},{3,4},{5,6},{2,1},{4,3},{6,5},{9,10},{11,12},{13,14},{10,9},... | collective-permute-start | bytes 786440 | tf_op jit(solution)/shard_map/while/body/eval_jaxpr/cond/branch_3_fun/ppermute | solution.py:326
  61.2 19.6 %collective-permute-start.39 = (f32[15,16,512]{2,1,0:T(8,128)S(1)}, f32[15,16,512]{2,1,0:T(8,128)S(1)}, u32[]{:S(2)}, u32[]{:S(2)}) collective-permute-start(f32[15,16,512]{2,1,0:T(8,128)S(1)} %get-tuple-element.399), channel_id=1, source_target_pairs={{8,16},{24,32},{40,48},{56,64},{72,80},{88,96},{104,112},{120,128}... | collective-permute-start | bytes 1474568 | tf_op jit(solution)/shard_map/while/body/eval_jaxpr/cond/branch_3_fun/ppermute | solution.py:326
  67.2 18.9 %collective-permute-start.38 = (f32[15,16,512]{2,1,0:T(8,128)S(1)}, f32[15,16,512]{2,1,0:T(8,128)S(1)}, u32[]{:S(2)}, u32[]{:S(2)}) collective-permute-start(f32[15,16,512]{2,1,0:T(8,128)S(1)} %get-tuple-element.396), channel_id=1, source_target_pairs={{8,16},{24,32},{40,48},{56,64},{72,80},{88,96},{104,112},{120,128}... | collective-permute-start | bytes 1474568 | tf_op jit(solution)/shard_map/while/body/eval_jaxpr/cond/branch_3_fun/ppermute | solution.py:326
  89.0 11.4 %collective-permute-start.11 = (f32[16,8,512]{2,1,0:T(8,128)S(1)}, f32[16,8,512]{2,1,0:T(8,128)S(1)}, u32[]{:S(2)}, u32[]{:S(2)}) collective-permute-start(f32[16,8,512]{2,1,0:T(8,128)S(1)} %get-tuple-element.322.e1_ref.other1_ref), channel_id=1, source_target_pairs={{1,2},{3,4},{5,6},{2,1},{4,3},{6,5},{9,10},{11,12},{13,14},{10,9},... | collective-permute-start | bytes 786440 | tf_op jit(solution)/shard_map/while/body/eval_jaxpr/cond/branch_1_fun/ppermute | solution.py:326
  101.5 19.3 %collective-permute-start.12 = (f32[9,32,512]{2,1,0:T(8,128)S(1)}, f32[9,32,512]{2,1,0:T(8,128)S(1)}, u32[]{:S(2)}, u32[]{:S(2)}) collective-permute-start(f32[9,32,512]{2,1,0:T(8,128)S(1)} %get-tuple-element.329), channel_id=1, source_target_pairs={{0,8},{16,24},{32,40},{48,56},{64,72},{80,88},{96,104},{112,120},{... | collective-permute-start | bytes 1769480 | tf_op jit(solution)/shard_map/while/body/eval_jaxpr/cond/branch_1_fun/ppermute | solution.py:326
  101.6 19.6 %collective-permute-start.14 = (f32[9,16,512]{2,1,0:T(8,128)S(1)}, f32[9,16,512]{2,1,0:T(8,128)S(1)}, u32[]{:S(2)}, u32[]{:S(2)}) collective-permute-start(f32[9,16,512]{2,1,0:T(8,128)S(1)} %get-tuple-element.331), channel_id=1, source_target_pairs={{8,16},{24,32},{40,48},{56,64},{72,80},{88,96},{104,112},{120,128}... | collective-permute-start | bytes 884744 | tf_op jit(solution)/shard_map/while/body/eval_jaxpr/cond/branch_1_fun/ppermute | solution.py:326
  128.0 12.4 %collective-permute-start.16 = (f32[16,8,512]{2,1,0:T(8,128)S(1)}, f32[16,8,512]{2,1,0:T(8,128)S(1)}, u32[]{:S(2)}, u32[]{:S(2)}) collective-permute-start(f32[16,8,512]{2,1,0:T(8,128)S(1)} %get-tuple-element.334.e1_ref), channel_id=1, source_target_pairs={{1,2},{3,4},{5,6},{2,1},{4,3},{6,5},{9,10},{11,12},{13,14},{10,9},... | collective-permute-start | bytes 786440 | tf_op jit(solution)/shard_map/while/body/eval_jaxpr/cond/branch_1_fun/ppermute | solution.py:326
  141.5 12.5 %collective-permute-start.17 = (f32[9,32,512]{2,1,0:T(8,128)S(1)}, f32[9,32,512]{2,1,0:T(8,128)S(1)}, u32[]{:S(2)}, u32[]{:S(2)}) collective-permute-start(f32[9,32,512]{2,1,0:T(8,128)S(1)} %get-tuple-element.337), channel_id=1, source_target_pairs={{0,8},{16,24},{32,40},{48,56},{64,72},{80,88},{96,104},{112,120},{... | collective-permute-start | bytes 1769480 | tf_op jit(solution)/shard_map/while/body/eval_jaxpr/cond/branch_1_fun/ppermute | solution.py:326
  141.6 14.9 %collective-permute-start.19 = (f32[9,16,512]{2,1,0:T(8,128)S(1)}, f32[9,16,512]{2,1,0:T(8,128)S(1)}, u32[]{:S(2)}, u32[]{:S(2)}) collective-permute-start(f32[9,16,512]{2,1,0:T(8,128)S(1)} %get-tuple-element.341), channel_id=1, source_target_pairs={{8,16},{24,32},{40,48},{56,64},{72,80},{88,96},{104,112},{120,128}... | collective-permute-start | bytes 884744 | tf_op jit(solution)/shard_map/while/body/eval_jaxpr/cond/branch_1_fun/ppermute | solution.py:326
  165.2 15.5 %collective-permute-start.11 = (f32[16,8,512]{2,1,0:T(8,128)S(1)}, f32[16,8,512]{2,1,0:T(8,128)S(1)}, u32[]{:S(2)}, u32[]{:S(2)}) collective-permute-start(f32[16,8,512]{2,1,0:T(8,128)S(1)} %get-tuple-element.322.e1_ref.other1_ref), channel_id=1, source_target_pairs={{1,2},{3,4},{5,6},{2,1},{4,3},{6,5},{9,10},{11,12},{13,14},{10,9},... | collective-permute-start | bytes 786440 | tf_op jit(solution)/shard_map/while/body/eval_jaxpr/cond/branch_1_fun/ppermute | solution.py:326
  181.8 12.1 %collective-permute-start.12 = (f32[9,32,512]{2,1,0:T(8,128)S(1)}, f32[9,32,512]{2,1,0:T(8,128)S(1)}, u32[]{:S(2)}, u32[]{:S(2)}) collective-permute-start(f32[9,32,512]{2,1,0:T(8,128)S(1)} %get-tuple-element.329), channel_id=1, source_target_pairs={{0,8},{16,24},{32,40},{48,56},{64,72},{80,88},{96,104},{112,120},{... | collective-permute-start | bytes 1769480 | tf_op jit(solution)/shard_map/while/body/eval_jaxpr/cond/branch_1_fun/ppermute | solution.py:326
  181.9 12.4 %collective-permute-start.14 = (f32[9,16,512]{2,1,0:T(8,128)S(1)}, f32[9,16,512]{2,1,0:T(8,128)S(1)}, u32[]{:S(2)}, u32[]{:S(2)}) collective-permute-start(f32[9,16,512]{2,1,0:T(8,128)S(1)} %get-tuple-element.331), channel_id=1, source_target_pairs={{8,16},{24,32},{40,48},{56,64},{72,80},{88,96},{104,112},{120,128}... | collective-permute-start | bytes 884744 | tf_op jit(solution)/shard_map/while/body/eval_jaxpr/cond/branch_1_fun/ppermute | solution.py:326
  201.1 15.5 %collective-permute-start.16 = (f32[16,8,512]{2,1,0:T(8,128)S(1)}, f32[16,8,512]{2,1,0:T(8,128)S(1)}, u32[]{:S(2)}, u32[]{:S(2)}) collective-permute-start(f32[16,8,512]{2,1,0:T(8,128)S(1)} %get-tuple-element.334.e1_ref), channel_id=1, source_target_pairs={{1,2},{3,4},{5,6},{2,1},{4,3},{6,5},{9,10},{11,12},{13,14},{10,9},... | collective-permute-start | bytes 786440 | tf_op jit(solution)/shard_map/while/body/eval_jaxpr/cond/branch_1_fun/ppermute | solution.py:326
  217.9 10.9 %collective-permute-start.19 = (f32[9,16,512]{2,1,0:T(8,128)S(1)}, f32[9,16,512]{2,1,0:T(8,128)S(1)}, u32[]{:S(2)}, u32[]{:S(2)}) collective-permute-start(f32[9,16,512]{2,1,0:T(8,128)S(1)} %get-tuple-element.341), channel_id=1, source_target_pairs={{8,16},{24,32},{40,48},{56,64},{72,80},{88,96},{104,112},{120,128}... | collective-permute-start | bytes 884744 | tf_op jit(solution)/shard_map/while/body/eval_jaxpr/cond/branch_1_fun/ppermute | solution.py:326
  237.5 19.8 %collective-permute-start.31 = (f32[16,8,512]{2,1,0:T(8,128)S(1)}, f32[16,8,512]{2,1,0:T(8,128)S(1)}, u32[]{:S(2)}, u32[]{:S(2)}) collective-permute-start(f32[16,8,512]{2,1,0:T(8,128)S(1)} %get-tuple-element.380.e1_ref.other1_ref), channel_id=1, source_target_pairs={{1,2},{3,4},{5,6},{2,1},{4,3},{6,5},{9,10},{11,12},{13,14},{10,9},... | collective-permute-start | bytes 786440 | tf_op jit(solution)/shard_map/while/body/eval_jaxpr/cond/branch_3_fun/ppermute | solution.py:326
  258.5 11.9 %collective-permute-start.32 = (f32[15,32,512]{2,1,0:T(8,128)S(1)}, f32[15,32,512]{2,1,0:T(8,128)S(1)}, u32[]{:S(2)}, u32[]{:S(2)}) collective-permute-start(f32[15,32,512]{2,1,0:T(8,128)S(1)} %get-tuple-element.387), channel_id=1, source_target_pairs={{0,8},{16,24},{32,40},{48,56},{64,72},{80,88},{96,104},{112,120},{... | collective-permute-start | bytes 2949128 | tf_op jit(solution)/shard_map/while/body/eval_jaxpr/cond/branch_3_fun/ppermute | solution.py:326
  258.6 13.2 %collective-permute-start.34 = (f32[15,16,512]{2,1,0:T(8,128)S(1)}, f32[15,16,512]{2,1,0:T(8,128)S(1)}, u32[]{:S(2)}, u32[]{:S(2)}) collective-permute-start(f32[15,16,512]{2,1,0:T(8,128)S(1)} %get-tuple-element.389), channel_id=1, source_target_pairs={{8,16},{24,32},{40,48},{56,64},{72,80},{88,96},{104,112},{120,128}... | collective-permute-start | bytes 1474568 | tf_op jit(solution)/shard_map/while/body/eval_jaxpr/cond/branch_3_fun/ppermute | solution.py:326
  265.3 12.3 %collective-permute-start.33 = (f32[15,16,512]{2,1,0:T(8,128)S(1)}, f32[15,16,512]{2,1,0:T(8,128)S(1)}, u32[]{:S(2)}, u32[]{:S(2)}) collective-permute-start(f32[15,16,512]{2,1,0:T(8,128)S(1)} %get-tuple-element.388), channel_id=1, source_target_pairs={{8,16},{24,32},{40,48},{56,64},{72,80},{88,96},{104,112},{120,128}... | collective-permute-start | bytes 1474568 | tf_op jit(solution)/shard_map/while/body/eval_jaxpr/cond/branch_3_fun/ppermute | solution.py:326
  291.2 20.5 %collective-permute-start.37 = (f32[15,32,512]{2,1,0:T(8,128)S(1)}, f32[15,32,512]{2,1,0:T(8,128)S(1)}, u32[]{:S(2)}, u32[]{:S(2)}) collective-permute-start(f32[15,32,512]{2,1,0:T(8,128)S(1)} %get-tuple-element.395), channel_id=1, source_target_pairs={{0,8},{16,24},{32,40},{48,56},{64,72},{80,88},{96,104},{112,120},{... | collective-permute-start | bytes 2949128 | tf_op jit(solution)/shard_map/while/body/eval_jaxpr/cond/branch_3_fun/ppermute | solution.py:326
  291.3 25.0 %collective-permute-start.39 = (f32[15,16,512]{2,1,0:T(8,128)S(1)}, f32[15,16,512]{2,1,0:T(8,128)S(1)}, u32[]{:S(2)}, u32[]{:S(2)}) collective-permute-start(f32[15,16,512]{2,1,0:T(8,128)S(1)} %get-tuple-element.399), channel_id=1, source_target_pairs={{8,16},{24,32},{40,48},{56,64},{72,80},{88,96},{104,112},{120,128}... | collective-permute-start | bytes 1474568 | tf_op jit(solution)/shard_map/while/body/eval_jaxpr/cond/branch_3_fun/ppermute | solution.py:326
  309.8 12.3 %collective-permute-start.38 = (f32[15,16,512]{2,1,0:T(8,128)S(1)}, f32[15,16,512]{2,1,0:T(8,128)S(1)}, u32[]{:S(2)}, u32[]{:S(2)}) collective-permute-start(f32[15,16,512]{2,1,0:T(8,128)S(1)} %get-tuple-element.396), channel_id=1, source_target_pairs={{8,16},{24,32},{40,48},{56,64},{72,80},{88,96},{104,112},{120,128}... | collective-permute-start | bytes 1474568 | tf_op jit(solution)/shard_map/while/body/eval_jaxpr/cond/branch_3_fun/ppermute | solution.py:326
  (41 other events, 739.3 us)
